TPU v7x, 32 devices: a whole 2x2x4 slice. The times are simulated.
32 devices in a mesh: rep: 4 (over x, core), fsdp: 8 (over z, y).
Axes of the slice: x: 2, y: 2, z: 4, core: 2. Of those that a mesh axis runs over, the one named last changes fastest.
Arguments:
- inputs: bfloat16 [2, 8192, 1024], P(None, ('rep', 'fsdp')), may hold values from -6 to 6
- cotangent: bfloat16 [2, 8192, 1024], P(None, ('rep', 'fsdp')), may hold values from -6 to 6
- lengths: int32 [2, 32], replicated, may hold values from 128 to 256, as said below
- norm_one: bfloat16 [1024], P('fsdp'), may hold values from 0.5 to 1.5
- w_in: bfloat16 [1024, 3072], P('fsdp'), may hold values from -0.1875 to 0.1875
- conv_w: bfloat16 [3, 1024], P(None, 'fsdp'), may hold values from -3.5 to 3.5
- w_out: bfloat16 [1024, 1024], P('fsdp'), may hold values from -0.1875 to 0.1875
- norm_two: bfloat16 [1024], P('fsdp'), may hold values from 0.5 to 1.5
- w_gate: bfloat16 [1024, 4608], P('fsdp'), may hold values from -0.1875 to 0.1875
- w_up: bfloat16 [1024, 4608], P('fsdp'), may hold values from -0.1875 to 0.1875
- w_down: bfloat16 [4608, 1024], P('fsdp'), may hold values from -0.125 to 0.125
Outputs:
- outputs: float32 [2, 8192, 1024], P(None, ('rep', 'fsdp'))
- d_inputs: float32 [2, 8192, 1024], P(None, ('rep', 'fsdp'))
- d_norm_one: float32 [1024], P('fsdp')
- d_w_in: float32 [1024, 3072], P('fsdp')
- d_conv_w: float32 [3, 1024], P(None, 'fsdp')
- d_w_out: float32 [1024, 1024], P('fsdp')
- d_norm_two: float32 [1024], P('fsdp')
- d_w_gate: float32 [1024, 4608], P('fsdp')
- d_w_up: float32 [1024, 4608], P('fsdp')
- d_w_down: float32 [4608, 1024], P('fsdp')
Inputs may be any that keep to these rules, and one draw needn't show every extreme that they name: `lengths`: in every micro-batch one slot holds exactly 256 live tokens and one exactly 128.
All inputs are finite; a program needn't handle non-finite values.
Results may differ from a plain program's by a relative error of at most 0.012.
Values may be sent and summed in bfloat16 or wider, within the bound.
A program may use at most 256 MiB of HBM per device.

v0:
```python
import jax
import jax.numpy as jnp
from jax import lax
from jax.sharding import PartitionSpec as P

EPSILON = 1e-05


def rms_scale(values):
    return lax.rsqrt(jnp.mean(values * values, axis=-1, keepdims=True) + EPSILON)


def dot_last(left, right):
    return lax.dot_general(
        left, right, (((1,), (1,)), ((), ())), preferred_element_type=jnp.float32
    )


def dot_first(left, right):
    return lax.dot_general(
        left, right, (((0,), (0,)), ((), ())), preferred_element_type=jnp.float32
    )


def norm_back(d_act, values, scale, gain):
    scaled = d_act * gain
    return scale * (
        scaled - values * scale * scale * jnp.mean(scaled * values, axis=-1, keepdims=True)
    )


def on_device(
    inputs, cotangent, lengths, norm_one, w_in, conv_w, w_out, norm_two, w_gate, w_up, w_down
):
    micro_count, tok_rows, features = inputs.shape
    shards = lax.axis_size("fsdp")
    fsdp_pos = lax.axis_index("fsdp")
    rep_pos = lax.axis_index("rep")
    slot_id = rep_pos * shards + fsdp_pos
    position = jnp.arange(tok_rows, dtype=jnp.int32)
    slot_cols = jnp.arange(lengths.shape[1], dtype=jnp.int32)
    shares = None
    results = []
    d_results = []
    for micro_step in range(micro_count):
        gathered = (
            lax.all_gather(norm_one, "fsdp", axis=0, tiled=True),
            lax.all_gather(w_in, "fsdp", axis=0, tiled=True),
            lax.all_gather(conv_w, "fsdp", axis=1, tiled=True),
            lax.all_gather(w_out, "fsdp", axis=0, tiled=True),
            lax.all_gather(norm_two, "fsdp", axis=0, tiled=True),
            lax.all_gather(w_gate, "fsdp", axis=0, tiled=True),
            lax.all_gather(w_up, "fsdp", axis=0, tiled=True),
            lax.all_gather(w_down, "fsdp", axis=0, tiled=True),
        )
        (
            forward_g_one,
            forward_m_in,
            forward_m_conv,
            forward_m_out,
            forward_g_two,
            forward_m_gate,
            forward_m_up,
            forward_m_down,
        ) = gathered
        forward_rows_f = inputs[micro_step].astype(jnp.float32)
        forward_scale_one = rms_scale(forward_rows_f)
        forward_act_one = (
            forward_rows_f * forward_scale_one * forward_g_one.astype(jnp.float32)
        ).astype(jnp.bfloat16)
        projected = jnp.dot(forward_act_one, forward_m_in, preferred_element_type=jnp.float32)
        forward_part_b = projected[:, :features]
        forward_part_c = projected[:, features : 2 * features]
        forward_part_x = projected[:, 2 * features :]
        product = forward_part_b * forward_part_x
        forward_padded = jnp.concatenate([jnp.zeros((2, features), jnp.float32), product], axis=0)
        forward_kernel = forward_m_conv.astype(jnp.float32)
        forward_convolved = (
            forward_kernel[0] * forward_padded[:-2]
            + forward_kernel[1] * forward_padded[1:-1]
            + forward_kernel[2] * forward_padded[2:]
        )
        forward_mixer_in = (forward_part_c * forward_convolved).astype(jnp.bfloat16)
        forward_hstate = forward_rows_f + jnp.dot(
            forward_mixer_in, forward_m_out, preferred_element_type=jnp.float32
        )
        forward_scale_two = rms_scale(forward_hstate)
        forward_act_two = (
            forward_hstate * forward_scale_two * forward_g_two.astype(jnp.float32)
        ).astype(jnp.bfloat16)
        forward_gate_pre = jnp.dot(
            forward_act_two, forward_m_gate, preferred_element_type=jnp.float32
        )
        forward_up_pre = jnp.dot(forward_act_two, forward_m_up, preferred_element_type=jnp.float32)
        forward_hidden = (jax.nn.silu(forward_gate_pre) * forward_up_pre).astype(jnp.bfloat16)
        result = forward_hstate + jnp.dot(
            forward_hidden, forward_m_down, preferred_element_type=jnp.float32
        )
        forward_kept_vals = (
            forward_rows_f,
            forward_scale_one,
            forward_act_one,
            forward_part_b,
            forward_part_c,
            forward_part_x,
            forward_padded,
            forward_convolved,
            forward_mixer_in,
            forward_hstate,
            forward_scale_two,
            forward_act_two,
            forward_gate_pre,
            forward_up_pre,
            forward_hidden,
        )
        result, kept_vals = (result, forward_kept_vals)
        gathered = (
            lax.all_gather(norm_one, "fsdp", axis=0, tiled=True),
            lax.all_gather(w_in, "fsdp", axis=0, tiled=True),
            lax.all_gather(conv_w, "fsdp", axis=1, tiled=True),
            lax.all_gather(w_out, "fsdp", axis=0, tiled=True),
            lax.all_gather(norm_two, "fsdp", axis=0, tiled=True),
            lax.all_gather(w_gate, "fsdp", axis=0, tiled=True),
            lax.all_gather(w_up, "fsdp", axis=0, tiled=True),
            lax.all_gather(w_down, "fsdp", axis=0, tiled=True),
        )
        length_now = jnp.sum(jnp.where(slot_cols == slot_id, lengths[micro_step], 0))
        live_rows = (position < length_now).astype(jnp.float32)[:, None]
        g_one, m_in, m_conv, m_out, g_two, m_gate, m_up, m_down = gathered
        (
            rows_f,
            scale_one,
            act_one,
            part_b,
            part_c,
            part_x,
            padded,
            convolved,
            mixer_in,
            hstate,
            scale_two,
            act_two,
            gate_pre,
            up_pre,
            hidden,
        ) = kept_vals
        cotan_f = cotangent[micro_step].astype(jnp.float32) * live_rows
        cotan_low = cotan_f.astype(jnp.bfloat16)
        d_hidden = dot_last(cotan_low, m_down)
        grad_down = dot_first(hidden, cotan_low)
        sigmoid_g = jax.nn.sigmoid(gate_pre)
        silu_g = gate_pre * sigmoid_g
        d_gate = (d_hidden * up_pre * sigmoid_g * (1.0 + gate_pre * (1.0 - sigmoid_g))).astype(
            jnp.bfloat16
        )
        d_up = (d_hidden * silu_g).astype(jnp.bfloat16)
        grad_gate = dot_first(act_two, d_gate)
        grad_up = dot_first(act_two, d_up)
        d_act_two = dot_last(d_gate, m_gate) + dot_last(d_up, m_up)
        grad_two = jnp.sum(d_act_two * hstate * scale_two, axis=0)
        d_hstate = cotan_f + norm_back(d_act_two, hstate, scale_two, g_two.astype(jnp.float32))
        d_mixer = d_hstate.astype(jnp.bfloat16)
        grad_out = dot_first(mixer_in, d_mixer)
        d_mixin = dot_last(d_mixer, m_out)
        d_cpart = d_mixin * convolved
        d_conv = d_mixin * part_c
        trailing = jnp.concatenate([d_conv, jnp.zeros((2, features), jnp.float32)], axis=0)
        kernel = m_conv.astype(jnp.float32)
        d_product = kernel[2] * d_conv + kernel[1] * trailing[1:-1] + kernel[0] * trailing[2:]
        grad_conv = jnp.stack(
            [
                jnp.sum(d_conv * padded[0:tok_rows], axis=0),
                jnp.sum(d_conv * padded[1 : tok_rows + 1], axis=0),
                jnp.sum(d_conv * padded[2 : tok_rows + 2], axis=0),
            ]
        )
        d_projected = jnp.concatenate(
            [d_product * part_x, d_cpart, d_product * part_b], axis=1
        ).astype(jnp.bfloat16)
        grad_in = dot_first(act_one, d_projected)
        d_act_one = dot_last(d_projected, m_in)
        grad_one = jnp.sum(d_act_one * rows_f * scale_one, axis=0)
        d_rows = d_hstate + norm_back(d_act_one, rows_f, scale_one, g_one.astype(jnp.float32))
        d_rows, grads = (
            d_rows,
            (grad_one, grad_in, grad_conv, grad_out, grad_two, grad_gate, grad_up, grad_down),
        )
        results.append(result)
        d_results.append(d_rows)
        piece_sums = (
            lax.psum_scatter(grads[0], "fsdp", scatter_dimension=0, tiled=True),
            lax.psum_scatter(grads[1], "fsdp", scatter_dimension=0, tiled=True),
            lax.psum_scatter(grads[2], "fsdp", scatter_dimension=1, tiled=True),
            lax.psum_scatter(grads[3], "fsdp", scatter_dimension=0, tiled=True),
            lax.psum_scatter(grads[4], "fsdp", scatter_dimension=0, tiled=True),
            lax.psum_scatter(grads[5], "fsdp", scatter_dimension=0, tiled=True),
            lax.psum_scatter(grads[6], "fsdp", scatter_dimension=0, tiled=True),
            lax.psum_scatter(grads[7], "fsdp", scatter_dimension=0, tiled=True),
        )
        shares = (
            piece_sums if shares is None else tuple((a + b for a, b in zip(shares, piece_sums)))
        )
    totals = (
        lax.psum(shares[0].astype(jnp.bfloat16), "rep").astype(jnp.float32),
        lax.psum(shares[1].astype(jnp.bfloat16), "rep").astype(jnp.float32),
        lax.psum(shares[2].astype(jnp.bfloat16), "rep").astype(jnp.float32),
        lax.psum(shares[3].astype(jnp.bfloat16), "rep").astype(jnp.float32),
        lax.psum(shares[4].astype(jnp.bfloat16), "rep").astype(jnp.float32),
        lax.psum(shares[5].astype(jnp.bfloat16), "rep").astype(jnp.float32),
        lax.psum(shares[6].astype(jnp.bfloat16), "rep").astype(jnp.float32),
        lax.psum(shares[7].astype(jnp.bfloat16), "rep").astype(jnp.float32),
    )
    outputs = jnp.stack(results)
    d_inputs = jnp.stack(d_results)
    return (
        outputs,
        d_inputs,
        totals[0],
        totals[1],
        totals[2],
        totals[3],
        totals[4],
        totals[5],
        totals[6],
        totals[7],
    )


def solution(mesh):
    return jax.shard_map(
        on_device,
        mesh=mesh,
        in_specs=(
            P(None, ("rep", "fsdp"), None),
            P(None, ("rep", "fsdp"), None),
            P(),
            P("fsdp"),
            P("fsdp", None),
            P(None, "fsdp"),
            P("fsdp", None),
            P("fsdp"),
            P("fsdp", None),
            P("fsdp", None),
            P("fsdp", None),
        ),
        out_specs=(
            P(None, ("rep", "fsdp"), None),
            P(None, ("rep", "fsdp"), None),
            P("fsdp"),
            P("fsdp", None),
            P(None, "fsdp"),
            P("fsdp", None),
            P("fsdp"),
            P("fsdp", None),
            P("fsdp", None),
            P("fsdp", None),
        ),
        check_vma=False,
    )
```

profile of v0, /device:TPU:0, one launch (start us, length us, event | category | flops | bytes accessed | tf_op | source)
XLA Modules:
  0.0 2069.6 jit_solution(8585196357545668894)
XLA Ops:
  10.7 22.4 %all-gather = bf16[8,1,128]{2,1,0:T(2,128)(2,1)S(1)} all-gather(bf16[1,1,128]{2,1,0:T(2,128)(2,1)S(1)} %bitcast.134), channel_id=1, replica_groups=mesh['rep'=4,'fsdp'=8] {'fsdp'}, dimensions={0}, use_global_device_ids=true | all-gather | bytes 2304 | tf_op jit(solution)/shard_map/all_gather | solution.py:47
  33.0 16.5 all-gather.1
  49.5 18.6 all_gather.18
  70.4 41.7 %all-gather.8.cloned.1.call-done = bf16[1024,3072]{1,0:T(8,128)(2,1)} async-done(((bf16[128,3072]{1,0:T(8,128)(2,1)}), bf16[1024,3072]{1,0:T(8,128)(2,1)}) %all-gather.8.cloned.1.call-update) | async-done | bytes 6291472 | tf_op jit(solution)/shard_map/all_gather | solution.py:48
  123.2 38.6 %all-gather.10.cloned.1.call-done = bf16[1024,1024]{1,0:T(8,128)(2,1)} async-done(((bf16[128,1024]{1,0:T(8,128)(2,1)}), bf16[1024,1024]{1,0:T(8,128)(2,1)}) %all-gather.10.cloned.1.call-update) | async-done | bytes 2097168 | tf_op jit(solution)/shard_map/all_gather | solution.py:50
  166.2 134.3 %all-gather.12.cloned.1.call-done = bf16[1024,4608]{1,0:T(8,128)(2,1)} async-done(((bf16[128,4608]{1,0:T(8,128)(2,1)}), bf16[1024,4608]{1,0:T(8,128)(2,1)}) %all-gather.12.cloned.1.call-update) | async-done | bytes 9437200 | tf_op jit(solution)/shard_map/all_gather | solution.py:52
  300.5 8.1 fusion.62
  308.7 130.2 %all-gather.14.cloned.1.call-done = bf16[1024,4608]{1,0:T(8,128)(2,1)} async-done(((bf16[128,4608]{1,0:T(8,128)(2,1)}), bf16[1024,4608]{1,0:T(8,128)(2,1)}) %all-gather.14.cloned.1.call-update) | async-done | bytes 9437200 | tf_op jit(solution)/shard_map/all_gather | solution.py:53
  438.8 7.9 fusion.63
  446.7 130.4 %all-gather.16.cloned.1.call-done = bf16[4608,1024]{1,0:T(8,128)(2,1)} async-done(((bf16[576,1024]{1,0:T(8,128)(2,1)}), bf16[4608,1024]{1,0:T(8,128)(2,1)}) %all-gather.16.cloned.1.call-update) | async-done | bytes 9437200 | tf_op jit(solution)/shard_map/all_gather | solution.py:54
  577.2 13.3 multiply_convert_fusion.2
  590.5 6.9 fusion.66
  597.4 8.3 multiply_reduce_fusion.1
  608.4 8.0 fusion.65
  616.3 13.8 multiply_convert_fusion
  657.9 6.4 convolution_add_fusion.3
  664.4 10.0 fusion.68
  674.4 12.5 convolution_add_fusion.2
  687.1 10.0 fusion.69
  697.2 12.2 convolution_add_fusion.1
  710.6 10.1 fusion.42
  720.6 12.3 convolution_add_fusion
  736.2 8.2 fusion.2
  751.8 190.8 %reduce-scatter.9.cloned.1.call-done = f32[128,3072]{1,0:T(8,128)} async-done(((f32[1024,3072]{1,0:T(8,128)}), f32[128,3072]{1,0:T(8,128)}) %reduce-scatter.9.cloned.1.call-update) | async-done | bytes 1572880 | tf_op jit(solution)/shard_map/reduce_scatter | solution.py:192
  945.0 314.4 %reduce-scatter.13.cloned.1.call-done = f32[128,4608]{1,0:T(8,128)} async-done(((f32[1024,4608]{1,0:T(8,128)}), f32[128,4608]{1,0:T(8,128)}) %reduce-scatter.13.cloned.1.call-update) | async-done | bytes 2359312 | tf_op jit(solution)/shard_map/reduce_scatter | solution.py:196
  1262.2 314.0 %reduce-scatter.15.cloned.1.call-done = f32[128,4608]{1,0:T(8,128)} async-done(((f32[1024,4608]{1,0:T(8,128)}), f32[128,4608]{1,0:T(8,128)}) %reduce-scatter.15.cloned.1.call-update) | async-done | bytes 2359312 | tf_op jit(solution)/shard_map/reduce_scatter | solution.py:197
  1579.0 313.9 %reduce-scatter.17.cloned.1.call-done = f32[576,1024]{1,0:T(8,128)} async-done(((f32[4608,1024]{1,0:T(8,128)}), f32[576,1024]{1,0:T(8,128)}) %reduce-scatter.17.cloned.1.call-update) | async-done | bytes 2359312 | tf_op jit(solution)/shard_map/reduce_scatter | solution.py:198
  1897.0 6.7 fusion.23
  1903.7 19.9 all-reduce.6
  1923.8 7.3 fusion.3
  1935.6 22.1 %reduce-scatter.19.cloned.1.call-done = f32[128,3]{1,0:T(8,128)} async-done(((f32[1024,3]{1,0:T(8,128)}), f32[128,3]{1,0:T(8,128)}) %reduce-scatter.19.cloned.1.call-update) | async-done | bytes 1552
  1965.9 87.2 %all-reduce.11.cloned.1.call-done = (bf16[128,3072]{1,0:T(8,128)(2,1)}, bf16[128,1024]{1,0:T(8,128)(2,1)}, bf16[128,4608]{1,0:T(8,128)(2,1)}, bf16[128,4608]{1,0:T(8,128)(2,1)}, bf16[576,1024]{1,0:T(8,128)(2,1)}) async-done(((bf16[128,3072]{1,0:T(8,128)(2,1)}, bf16[128,1024]{1,0:T(8,128)(2,1)}, bf16[128,4608]{1,0:T(8,128)(2,1)}, bf16[128,4608]{1,0:T(8,128)(2,1)}, bf16[576,1024]{1,0:T(8,128)(2,1)}), ...) | async-done | bytes 4587536 | tf_op jit(solution)/shard_map/psum | solution.py:205
  (198 shorter events, 96.7 us)
Async XLA Ops:
  7.2 25.9 %copy-start.50 = (bf16[128]{0:T(256)(128)(2,1)S(1)}, bf16[128]{0:T(256)(128)(2,1)}, u32[]{:S(2)}) copy-start(bf16[128]{0:T(256)(128)(2,1)} %param.18) | copy-start | bytes 772
  7.2 42.3 %copy-start.47 = (bf16[3,128]{1,0:T(4,128)(2,1)S(1)}, bf16[3,128]{1,0:T(4,128)(2,1)}, u32[]{:S(2)}) copy-start(bf16[3,128]{1,0:T(4,128)(2,1)} %param.16) | copy-start | bytes 2308
  7.2 60.9 %copy-start.48 = (s32[2,32]{1,0:T(2,128)S(1)}, s32[2,32]{1,0:T(2,128)}, u32[]{:S(2)}) copy-start(s32[2,32]{1,0:T(2,128)} %param.13) | copy-start | bytes 772
  7.2 62.9 %copy-start.4 = (bf16[2,256,1024]{2,1,0:T(8,128)(2,1)S(1)}, bf16[2,256,1024]{2,1,0:T(8,128)(2,1)}, u32[]{:S(2)}) copy-start(bf16[2,256,1024]{2,1,0:T(8,128)(2,1)} %param.11) | copy-start | bytes 3145732
  7.2 104.9 %all-gather.8.cloned.1.call-start = ((), (), s32[]{:S(2)}) async-start(), calls=%async_computation.6 | async-start | bytes 7077888 | tf_op jit(solution)/shard_map/all_gather | solution.py:48
  8.0 153.8 %all-gather.10.cloned.1.call-start = ((), (), s32[]{:S(2)}) async-start(), calls=%async_computation.7 | async-start | bytes 2359296 | tf_op jit(solution)/shard_map/all_gather | solution.py:50
  8.7 291.8 %all-gather.12.cloned.1.call-start = ((), (), s32[]{:S(2)}) async-start(), calls=%async_computation.8 | async-start | bytes 10616832 | tf_op jit(solution)/shard_map/all_gather | solution.py:52
  9.4 429.4 %all-gather.14.cloned.1.call-start = ((), (), s32[]{:S(2)}) async-start(), calls=%async_computation.9 | async-start | bytes 10616832 | tf_op jit(solution)/shard_map/all_gather | solution.py:53
  10.0 567.1 %all-gather.16.cloned.1.call-start = ((), (), s32[]{:S(2)}) async-start(), calls=%async_computation.10 | async-start | bytes 10616832 | tf_op jit(solution)/shard_map/all_gather | solution.py:54
  10.6 739.4 %reduce-scatter.11.cloned.1.call-start = ((), (), s32[]{:S(2)}) async-start(), calls=%async_computation.12 | async-start | bytes 4718592 | tf_op jit(solution)/shard_map/reduce_scatter | solution.py:194
  123.2 42.9 %copy-start.33 = (bf16[256,1024]{1,0:T(8,128)(2,1)}, bf16[256,1024]{1,0:T(8,128)(2,1)S(1)}, u32[]{:S(2)}) copy-start(bf16[256,1024]{1,0:T(8,128)(2,1)S(1)} %get-tuple-element.64) | copy-start | bytes 1572868
  123.2 42.9 %copy-start.35 = (bf16[256,1024]{1,0:T(8,128)(2,1)}, bf16[256,1024]{1,0:T(8,128)(2,1)S(1)}, u32[]{:S(2)}) copy-start(bf16[256,1024]{1,0:T(8,128)(2,1)S(1)} %get-tuple-element.46) | copy-start | bytes 1572868
  164.3 433.1 %copy-start.16 = (f32[256,1024]{1,0:T(8,128)}, f32[256,1024]{1,0:T(8,128)S(1)}, u32[]{:S(2)}) copy-start(f32[256,1024]{1,0:T(8,128)S(1)} %get-tuple-element.71) | copy-start | bytes 3145732
  308.7 268.5 %copy-start.13 = (bf16[2,256,1024]{2,1,0:T(8,128)(2,1)S(1)}, bf16[2,256,1024]{2,1,0:T(8,128)(2,1)}, u32[]{:S(2)}) copy-start(bf16[2,256,1024]{2,1,0:T(8,128)(2,1)} %param.12) | copy-start | bytes 3145732
  590.4 7.0 copy-start.19
  590.4 7.0 copy-start.40
  590.4 15.3 slice-start
  590.4 15.3 slice-start.1
  597.4 8.3 slice-start.2
  645.1 297.6 %reduce-scatter.9.cloned.1.call-start = ((), (), s32[]{:S(2)}) async-start(), calls=%async_computation.11 | async-start | bytes 14155776 | tf_op jit(solution)/shard_map/reduce_scatter | solution.py:192
  664.3 595.1 %reduce-scatter.13.cloned.1.call-start = ((), (), s32[]{:S(2)}) async-start(), calls=%async_computation.13 | async-start | bytes 21233664 | tf_op jit(solution)/shard_map/reduce_scatter | solution.py:196
  664.4 10.0 copy-start.23
  686.9 889.3 %reduce-scatter.15.cloned.1.call-start = ((), (), s32[]{:S(2)}) async-start(), calls=%async_computation.14 | async-start | bytes 21233664 | tf_op jit(solution)/shard_map/reduce_scatter | solution.py:197
  687.1 10.0 copy-start.22
  709.4 1183.6 %reduce-scatter.17.cloned.1.call-start = ((), (), s32[]{:S(2)}) async-start(), calls=%async_computation.15 | async-start | bytes 21233664 | tf_op jit(solution)/shard_map/reduce_scatter | solution.py:198
  710.6 10.1 copy-start.12
  733.0 1224.8 %reduce-scatter.19.cloned.1.call-start = ((), (), s32[]{:S(2)}) async-start(), calls=%async_computation.16 | async-start | bytes 589824
  735.9 8.5 copy-start.25
  735.9 8.5 copy-start.27
  736.0 1317.2 %all-reduce.11.cloned.1.call-start = ((), (), s32[]{:S(2)}) async-start(), calls=%async_computation.17 | async-start | bytes 9175040 | tf_op jit(solution)/shard_map/psum | solution.py:205
  736.2 8.2 copy-start.29
  1923.8 7.3 copy-start.44
  (36 other events, 129.7 us)
Sparse Core Ops, SparseCore 0:
  10.2 101.8 all-gather.7
  114.2 47.4 all-gather.9
  163.9 136.5 all-gather.11
  302.6 136.2 all-gather.13
  440.9 136.2 all-gather.15
  645.2 86.2 reduce-scatter.10
  735.5 207.0 reduce-scatter.8
  947.0 312.3 reduce-scatter.12
  1263.8 312.3 reduce-scatter.14
  1580.5 312.4 reduce-scatter.16
  1896.7 61.0 reduce-scatter.18
  1961.5 91.6 all-reduce.10
where the time goes:
time: 2080 us; the launch traced here: 2070 us
  waiting for transfers between devices  1720 us (83%)
  matrix products  202 us (10%)
  blocking collectives  83 us (4%)
  other arithmetic  34 us (2%)
    reduce_scatter x1, waiting for transfers between devices, on_device(): lax.psum_scatter(grads[5], 'fsdp', scatter_dimension=0, tiled=True)  314 us
    reduce_scatter x1, waiting for transfers between devices, on_device(): lax.psum_scatter(grads[6], 'fsdp', scatter_dimension=0, tiled=True)  314 us
    reduce_scatter x1, waiting for transfers between devices, on_device(): lax.psum_scatter(grads[7], 'fsdp', scatter_dimension=0, tiled=True)  314 us
    reduce_scatter x1, waiting for transfers between devices, on_device(): lax.psum_scatter(grads[1], 'fsdp', scatter_dimension=0, tiled=True)  191 us
    all_gather x1, waiting for transfers between devices, on_device(): lax.all_gather(w_gate, 'fsdp', axis=0, tiled=True)  134 us
    all_gather x1, waiting for transfers between devices, on_device(): lax.all_gather(w_down, 'fsdp', axis=0, tiled=True)  130 us
    all_gather x1, waiting for transfers between devices, on_device(): lax.all_gather(w_up, 'fsdp', axis=0, tiled=True)  130 us
    psum x1, waiting for transfers between devices, on_device(): lax.psum(shares[1].astype(jnp.bfloat16), 'rep').astype(jnp.float32)  87.2 us
  transfers between devices with their start and end apart: 12, of which 11 were waited for; matrix products, arithmetic and copies ran while one was open for 8% of the time, Pallas kernels for 0%

commit v1 on v0

v1 whole, which is shorter than its diff:
```python
import jax
import jax.numpy as jnp
from jax import lax
from jax.sharding import PartitionSpec as P

EPSILON = 1e-05
LOW = jnp.bfloat16
F32 = jnp.float32


def hop(values, axis, bit):
    size = lax.axis_size(axis)
    return lax.ppermute(values, axis, [(at, at ^ bit) for at in range(size)])


def after(values, *earlier):
    return lax.optimization_barrier((values, *earlier))[0]


def gather_bits():
    size = lax.axis_size("fsdp")
    bits = [1 << k for k in range(size.bit_length() - 1)]
    return bits[1:] + bits[:1]


def gather_pieces(own):
    pieces = {0: own}
    for bit in gather_bits():
        for offset in list(pieces):
            pieces[offset ^ bit] = hop(pieces[offset], "fsdp", bit)
    return pieces


def put(target, block, index):
    return lax.dynamic_update_slice(target, block, index + (0,) * (target.ndim - len(index)))


def in_order(pieces, place):
    shards = len(pieces)
    whole = jnp.zeros((shards, *pieces[0].shape), pieces[0].dtype)
    for offset, piece in pieces.items():
        whole = put(whole, piece[None], (place ^ offset,))
    return whole


def reduce_pieces(whole, kind=LOW):
    place = lax.axis_index("fsdp")
    shards = whole.shape[0]
    bits = gather_bits()[::-1]
    top = shards.bit_length() - 1
    rest = whole.shape[1:]
    held = whole.reshape((2,) * top + rest)
    axes = [1 << k for k in reversed(range(top))]
    for bit in bits:
        axis = axes.index(bit)
        mine = jnp.where((place & bit) != 0, 1, 0)
        sent = lax.dynamic_index_in_dim(held, 1 - mine, axis, keepdims=False).astype(kind)
        kept = lax.dynamic_index_in_dim(held, mine, axis, keepdims=False).astype(F32)
        total = kept + hop(sent, "fsdp", bit).astype(F32)
        axes.pop(axis)
        held = total.astype(kind) if axes else total
    return held


def rms_scale(values):
    return lax.rsqrt(jnp.mean(values * values, axis=-1, keepdims=True) + EPSILON)


def dot(left, right):
    return jnp.dot(left, right, preferred_element_type=F32)


def dot_last(left, right):
    return lax.dot_general(left, right, (((1,), (1,)), ((), ())), preferred_element_type=F32)


def dot_first(left, right):
    return lax.dot_general(left, right, (((0,), (0,)), ((), ())), preferred_element_type=F32)


def norm_back(d_act, values, scale, gain):
    scaled = d_act * gain
    return scale * (
        scaled - values * scale * scale * jnp.mean(scaled * values, axis=-1, keepdims=True)
    )


def sum_over_rep(own_and_core, across):
    rows = own_and_core.shape[0] // 2
    near = hop(own_and_core[rows:].astype(LOW), "rep", 1).astype(F32)
    far = hop(across[rows:].astype(LOW), "rep", 1).astype(F32)
    own = own_and_core[:rows] + near
    other = (across[:rows] + far).astype(LOW)
    return own + hop(other, "rep", 2).astype(F32)


def spread_over_rep(values):
    near = hop(values, "rep", 1)
    across = hop(values, "rep", 2)
    return jnp.concatenate([values, near]), jnp.concatenate([across, hop(across, "rep", 1)])


def share_quarters(quarter):
    rep = lax.axis_index("rep")
    near = hop(quarter, "rep", 1)
    across = hop(quarter, "rep", 2)
    corner = hop(across, "rep", 1)
    whole = jnp.zeros((4, *quarter.shape), quarter.dtype)
    for offset, block in enumerate((quarter, near, across, corner)):
        whole = put(whole, block[None], (rep ^ offset,))
    return whole


def gather_full(weight, *earlier):
    rep = lax.axis_index("rep")
    place = lax.axis_index("fsdp")
    rows, cols = weight.shape
    quarter = rows // 4
    own = lax.dynamic_slice_in_dim(weight, rep * quarter, quarter, 0)
    pieces = gather_pieces(after(own, *earlier) if earlier else own)
    shards = len(pieces)
    whole = jnp.zeros((shards, 4, quarter, cols), weight.dtype)
    whole = put(whole, weight.reshape(1, 4, quarter, cols), (place,))
    for flip in (0, 1):
        group = {o: p for o, p in pieces.items() if o & 1 == flip and o}
        offsets = sorted(group)
        stacked = jnp.stack([group[o] for o in offsets])
        across = hop(stacked, "rep", 2)
        near = hop(stacked, "rep", 1)
        corner = hop(across, "rep", 1)
        for turn, block in enumerate((stacked, near, across, corner)):
            for at, offset in enumerate(offsets):
                whole = put(whole, block[at][None, None], (place ^ offset, rep ^ turn))
    return whole.reshape(shards * rows, cols), pieces


def reduce_full(grad):
    rep = lax.axis_index("rep")
    shards = lax.axis_size("fsdp")
    rows, cols = grad.shape
    quarter = rows // shards // 4
    held = grad.reshape(shards, 2, 2, quarter, cols)
    core, side = rep & 1, (rep >> 1) & 1
    sent = lax.dynamic_index_in_dim(held, 1 - core, 2, keepdims=False).astype(LOW)
    kept = lax.dynamic_index_in_dim(held, core, 2, keepdims=False)
    pair = (kept.astype(F32) + hop(sent, "rep", 1).astype(F32)).astype(LOW)
    sent = lax.dynamic_index_in_dim(pair, 1 - side, 1, keepdims=False)
    kept = lax.dynamic_index_in_dim(pair, side, 1, keepdims=False)
    four = kept.astype(F32) + hop(sent, "rep", 2).astype(F32)
    own = reduce_pieces(four).astype(LOW)
    return share_quarters(own).reshape(4 * quarter, cols).astype(F32)


def on_device(
    inputs, cotangent, lengths, norm_one, w_in, conv_w, w_out, norm_two, w_gate, w_up, w_down
):
    micro_count, tok_rows, features = inputs.shape
    shards = lax.axis_size("fsdp")
    place = lax.axis_index("fsdp")
    rep = lax.axis_index("rep")
    all_rows = micro_count * tok_rows
    hidden_own = w_down.shape[0]
    cut = hidden_own // 4
    part_ff = shards * cut

    small = jnp.concatenate([norm_one[None], norm_two[None], conv_w, jnp.zeros_like(conv_w)])
    small_all = in_order(gather_pieces(small), place)
    small_all = jnp.moveaxis(small_all, 0, 1).reshape(8, features).astype(F32)
    g_one, g_two, taps = small_all[0], small_all[1], small_all[2:5]

    m_in, in_pieces = gather_full(w_in)
    m_out, out_pieces = gather_full(w_out, in_pieces[2])
    gate_own = lax.dynamic_index_in_dim(
        w_gate.reshape(-1, shards, 4, cut), rep, 2, keepdims=False
    ).reshape(-1, part_ff)
    up_own = lax.dynamic_index_in_dim(
        w_up.reshape(-1, shards, 4, cut), rep, 2, keepdims=False
    ).reshape(-1, part_ff)
    down_own = lax.dynamic_slice_in_dim(w_down, rep * cut, cut, 0)
    gate_pieces = gather_pieces(after(gate_own, in_pieces[4]))
    up_pieces = gather_pieces(after(up_own, gate_pieces[4]))
    down_pieces = gather_pieces(after(down_own, up_pieces[4]))
    m_gate = in_order(gate_pieces, place).reshape(features, part_ff)
    m_up = in_order(up_pieces, place).reshape(features, part_ff)
    m_down = in_order(down_pieces, place).reshape(part_ff, features)

    slot_cols = jnp.arange(lengths.shape[1], dtype=jnp.int32)
    slot_id = rep * shards + place
    length_now = jnp.sum(jnp.where(slot_cols == slot_id, lengths, 0), axis=1)
    position = jnp.arange(tok_rows, dtype=jnp.int32)
    live = (position[None] < length_now[:, None]).astype(F32)[..., None]
    cotan_f = (cotangent.astype(F32) * live).reshape(all_rows, features)
    cotan_low = cotan_f.astype(LOW)
    cot_near, cot_far = spread_over_rep(after(cotan_low, in_pieces[1]))

    rows_f = inputs.reshape(all_rows, features).astype(F32)
    scale_one = rms_scale(rows_f)
    act_one = (rows_f * scale_one * g_one).astype(LOW)
    projected = dot(act_one, m_in)
    part_b = projected[:, :features]
    part_c = projected[:, features : 2 * features]
    part_x = projected[:, 2 * features :]
    product = (part_b * part_x).reshape(micro_count, tok_rows, features)
    padded = jnp.pad(product, ((0, 0), (2, 0), (0, 0)))
    convolved = (
        taps[0] * padded[:, :-2] + taps[1] * padded[:, 1:-1] + taps[2] * padded[:, 2:]
    ).reshape(all_rows, features)
    mixer_in = (part_c * convolved).astype(LOW)
    hstate = rows_f + dot(mixer_in, m_out)
    scale_two = rms_scale(hstate)
    act_two = (hstate * scale_two * g_two).astype(LOW)
    act_near, act_far = spread_over_rep(act_two)

    def units(act, cot):
        gate_pre = dot(act, m_gate)
        up_pre = dot(act, m_up)
        sigmoid_g = jax.nn.sigmoid(gate_pre)
        silu_g = gate_pre * sigmoid_g
        hidden = (silu_g * up_pre).astype(LOW)
        d_hidden = dot_last(cot, m_down)
        d_gate = (d_hidden * up_pre * sigmoid_g * (1.0 + gate_pre * (1.0 - sigmoid_g))).astype(LOW)
        d_up = (d_hidden * silu_g).astype(LOW)
        return hidden, d_gate, d_up

    hidden_n, d_gate_n, d_up_n = units(act_near, cot_near)
    hidden_f, d_gate_f, d_up_f = units(act_far, cot_far)
    grad_down = dot_first(hidden_n, cot_near) + dot_first(hidden_f, cot_far)
    d_act_two = sum_over_rep(
        dot_last(d_gate_n, m_gate) + dot_last(d_up_n, m_up),
        dot_last(d_gate_f, m_gate) + dot_last(d_up_f, m_up),
    )
    grad_gate = dot_first(act_near, d_gate_n) + dot_first(act_far, d_gate_f)
    grad_up = dot_first(act_near, d_up_n) + dot_first(act_far, d_up_f)
    ffn = sum_over_rep(dot(hidden_n, m_down), dot(hidden_f, m_down))
    outputs = (hstate + ffn).reshape(inputs.shape)

    sum_down = reduce_pieces(grad_down.reshape(shards, cut, features))
    sum_gate = reduce_pieces(grad_gate.reshape(shards, -1, part_ff))
    sum_up = reduce_pieces(grad_up.reshape(shards, -1, part_ff))
    all_down = share_quarters(sum_down.astype(LOW)).reshape(hidden_own, features).astype(F32)

    def unit_columns(total):
        quarters = share_quarters(total.astype(LOW)).reshape(4, -1, shards, cut)
        return quarters.transpose(1, 2, 0, 3).reshape(-1, 4 * part_ff).astype(F32)

    all_gate = unit_columns(sum_gate)
    all_up = unit_columns(sum_up)

    grad_two = jnp.sum(d_act_two * hstate * scale_two, axis=0)
    d_hstate = cotan_f + norm_back(d_act_two, hstate, scale_two, g_two)
    d_mixer = d_hstate.astype(LOW)
    grad_out = dot_first(mixer_in, d_mixer)
    d_mixin = dot_last(d_mixer, m_out)
    d_cpart = d_mixin * convolved
    d_conv = (d_mixin * part_c).reshape(micro_count, tok_rows, features)
    trailing = jnp.pad(d_conv, ((0, 0), (0, 2), (0, 0)))
    d_product = (
        taps[2] * d_conv + taps[1] * trailing[:, 1:-1] + taps[0] * trailing[:, 2:]
    ).reshape(all_rows, features)
    grad_conv = [
        jnp.sum(d_conv * padded[:, k : k + tok_rows], axis=(0, 1)) for k in range(3)
    ]
    d_projected = jnp.concatenate(
        [d_product * part_x, d_cpart, d_product * part_b], axis=1
    ).astype(LOW)
    grad_in = dot_first(act_one, d_projected)
    d_act_one = dot_last(d_projected, m_in)
    grad_one = jnp.sum(d_act_one * rows_f * scale_one, axis=0)
    d_rows = d_hstate + norm_back(d_act_one, rows_f, scale_one, g_one)
    d_inputs = d_rows.reshape(inputs.shape)

    all_out = reduce_full(grad_out)
    all_in = reduce_full(grad_in)

    zeros = jnp.zeros_like(grad_one)
    small_grads = jnp.stack([grad_one, grad_two, *grad_conv, zeros, zeros, zeros])
    small_grads = jnp.moveaxis(small_grads.reshape(8, shards, -1), 1, 0)
    small_own = reduce_pieces(small_grads, F32)
    small_own = small_own + hop(small_own, "rep", 1)
    small_own = small_own + hop(small_own, "rep", 2)

    return (
        outputs,
        d_inputs,
        small_own[0],
        all_in,
        small_own[2:5],
        all_out,
        small_own[1],
        all_gate,
        all_up,
        all_down,
    )


def solution(mesh):
    return jax.shard_map(
        on_device,
        mesh=mesh,
        in_specs=(
            P(None, ("rep", "fsdp"), None),
            P(None, ("rep", "fsdp"), None),
            P(),
            P("fsdp"),
            P("fsdp", None),
            P(None, "fsdp"),
            P("fsdp", None),
            P("fsdp"),
            P("fsdp", None),
            P("fsdp", None),
            P("fsdp", None),
        ),
        out_specs=(
            P(None, ("rep", "fsdp"), None),
            P(None, ("rep", "fsdp"), None),
            P("fsdp"),
            P("fsdp", None),
            P(None, "fsdp"),
            P("fsdp", None),
            P("fsdp"),
            P("fsdp", None),
            P("fsdp", None),
            P("fsdp", None),
        ),
        check_vma=False,
    )
```

time: 2080 us -> 747 us (0.36)
  waiting for transfers between devices: 1720 us -> 302 us
  local copies, waits for them, and re-layouts: 12.2 us -> 166 us
  starting transfers between devices: 1.33 us -> 87.9 us
  blocking collectives: 83 us -> 0 us
  matrix products: 202 us -> 130 us
    reduce_scatter x5 -> x0, waiting for transfers between devices: 1130 us -> none  [the longest x1 314 us: on_device(): lax.psum_scatter(grads[5], 'fsdp', scatter_dimension=0, tiled=True)]
    all_gather x5 -> x0, waiting for transfers between devices: 475 us -> none  [the longest x1 134 us: on_device(): lax.all_gather(w_gate, 'fsdp', axis=0, tiled=True)]
    ppermute x0 -> x105, waiting for transfers between devices: none -> 302 us  [hop(): return lax.ppermute(values, axis, [(at, at ^ bit) for at in range(size)])]
    ppermute x0 -> x105, starting transfers between devices: none -> 87.9 us  [hop(): return lax.ppermute(values, axis, [(at, at ^ bit) for at in range(size)])]
    psum x1 -> x0, waiting for transfers between devices: 87.2 us -> none  [on_device(): lax.psum(shares[1].astype(jnp.bfloat16), 'rep').astype(jnp.float32)]
    dynamic_update_slice x0 -> x103, local copies, waits for them, and re-layouts: none -> 83.1 us  [put(): lax.dynamic_update_slice(target, block, index + (0,) * (target.ndim - len...]
    all_gather x3 -> x0, blocking collectives: 57.4 us -> none  [the longest x1 22.4 us: on_device(): lax.all_gather(norm_one, 'fsdp', axis=0, tiled=True)]
    dot_general x10 -> x8, matrix products: 79 us -> 32.8 us  [dot_first(): lax.dot_general(left, right, (((0,), (0,)), ((), ())), preferred_element_...]
  transfers between devices with their start and end apart: 12 -> 105, of which waited for: 11 -> 42; matrix products, arithmetic and copies ran while one was open for 8% -> 45% of each run, Pallas kernels for 0% -> 0%
where the time goes in v1:
time: 747 us; the launch traced here: 736 us
  waiting for transfers between devices  302 us (40%)
  local copies, waits for them, and re-layouts  166 us (22%)
  matrix products  130 us (17%)
  starting transfers between devices  87.9 us (12%)
  other arithmetic  46.7 us (6%)
    ppermute x105, waiting for transfers between devices, hop(): return lax.ppermute(values, axis, [(at, at ^ bit) for at in range(size)])  302 us
    ppermute x105, starting transfers between devices, hop(): return lax.ppermute(values, axis, [(at, at ^ bit) for at in range(size)])  87.9 us
    dynamic_update_slice x103, local copies, waits for them, and re-layouts, put(): lax.dynamic_update_slice(target, block, index + (0,) * (target.ndim - len...  83.1 us
    dot_general x8, matrix products, dot(): return jnp.dot(left, right, preferred_element_type=F32)  54 us
    dot_general x8, matrix products, dot_last(): lax.dot_general(left, right, (((1,), (1,)), ((), ())), preferred_element_...  43.4 us
    dot_general x8, matrix products, dot_first(): lax.dot_general(left, right, (((0,), (0,)), ((), ())), preferred_element_...  32.8 us
    unnamed x190, local copies, waits for them, and re-layouts  28.9 us
  transfers between devices with their start and end apart: 105, of which 42 were waited for; matrix products, arithmetic and copies ran while one was open for 45% of the time, Pallas kernels for 0%

profile of v1, /device:TPU:0, one launch (start us, length us, event | category | flops | bytes accessed | tf_op | source)
XLA Modules:
  0.0 735.7 jit_solution(3679388588807048803)
XLA Ops:
  64.7 9.9 %collective-permute-done.22 = bf16[32,1024]{1,0:T(8,128)(2,1)S(1)} collective-permute-done((bf16[32,1024]{1,0:T(8,128)(2,1)S(1)}, bf16[32,1024]{1,0:T(8,128)(2,1)S(1)}, u32[]{:S(2)}, u32[]{:S(2)}) %collective-permute-start.22) | collective-permute-done | bytes 65568 | tf_op jit(solution)/shard_map/ppermute | solution.py:13
  126.1 16.2 %collective-permute-done.36 = bf16[128,1152]{0,1:T(8,128)(2,1)S(1)} collective-permute-done((bf16[128,1152]{0,1:T(8,128)(2,1)}, bf16[128,1152]{0,1:T(8,128)(2,1)S(1)}, u32[]{:S(2)}, u32[]{:S(2)}) %collective-permute-start.36) | collective-permute-done | bytes 294944 | tf_op jit(solution)/shard_map/ppermute | solution.py:13
  180.2 9.5 %collective-permute-done.43 = bf16[128,1152]{1,0:T(8,128)(2,1)S(1)} collective-permute-done((bf16[128,1152]{1,0:T(8,128)(2,1)}, bf16[128,1152]{1,0:T(8,128)(2,1)S(1)}, u32[]{:S(2)}, u32[]{:S(2)}) %collective-permute-start.43) | collective-permute-done | bytes 294944 | tf_op jit(solution)/shard_map/ppermute | solution.py:13
  192.9 6.1 collective-permute-done.45
  202.5 6.4 collective-permute-done.40
  222.0 7.0 collective-permute-done.50
  232.5 6.5 collective-permute-done.52
  271.5 5.8 fusion.117
  291.4 5.3 fusion.123
  301.3 19.0 %multiply_convert_fusion.3 = (bf16[1024,1152]{1,0:T(8,128)(2,1)}, bf16[1024,1152]{1,0:T(8,128)(2,1)}, bf16[1024,1152]{1,0:T(8,128)(2,1)S(1)}) fusion(f32[1024,1152]{1,0:T(8,128)S(1)} %fusion.121, f32[1024,1152]{1,0:T(8,128)S(1)} %fusion.109, bf16[1024,1152]{1,0:T(8,128)(2,1)} %bitcast.104, bf16[512,1024]{1,0:T(8,128)(2,1)S(1)} %collective-permute-done.33, ...), kind=kOutput, calls=%fused_computation.6 | convolution fusion | flops 2437808128 | bytes 20971520 | tf_op jit(solution)/shard_map/dot_general | solution.py:70
  320.3 5.4 fusion.122
  331.8 4.7 fusion.118
  351.9 5.3 fusion.119
  357.3 6.7 multiply_convert_fusion.1
  364.0 6.3 fusion.124
  392.8 6.9 convolution_add_fusion.2
  431.1 19.0 %collective-permute-done.87 = bf16[2,2,128,1152]{2,3,1,0:T(8,128)(2,1)S(1)} collective-permute-done((bf16[2,2,128,1152]{2,3,1,0:T(8,128)(2,1)}, bf16[2,2,128,1152]{2,3,1,0:T(8,128)(2,1)S(1)}, u32[]{:S(2)}, u32[]{:S(2)}) %collective-permute-start.87) | collective-permute-done | bytes 1179680 | tf_op jit(solution)/shard_map/ppermute | solution.py:13
  450.4 24.3 %collective-permute-done.99 = bf16[2,2,144,1024]{3,2,1,0:T(8,128)(2,1)S(1)} collective-permute-done((bf16[2,2,144,1024]{3,2,1,0:T(8,128)(2,1)S(1)}, bf16[2,2,144,1024]{3,2,1,0:T(8,128)(2,1)S(1)}, u32[]{:S(2)}, u32[]{:S(2)}) %collective-permute-start.99) | collective-permute-done | bytes 1179680 | tf_op jit(solution)/shard_map/ppermute | solution.py:13
  478.4 35.1 %collective-permute-done.88 = bf16[2,128,1152]{1,2,0:T(8,128)(2,1)S(1)} collective-permute-done((bf16[2,128,1152]{1,2,0:T(8,128)(2,1)S(1)}, bf16[2,128,1152]{1,2,0:T(8,128)(2,1)S(1)}, u32[]{:S(2)}, u32[]{:S(2)}) %collective-permute-start.88) | collective-permute-done | bytes 589856 | tf_op jit(solution)/shard_map/ppermute | solution.py:13
  514.2 11.9 %collective-permute-done.100 = bf16[2,144,1024]{2,1,0:T(8,128)(2,1)S(1)} collective-permute-done((bf16[2,144,1024]{2,1,0:T(8,128)(2,1)S(1)}, bf16[2,144,1024]{2,1,0:T(8,128)(2,1)S(1)}, u32[]{:S(2)}, u32[]{:S(2)}) %collective-permute-start.100) | collective-permute-done | bytes 589856 | tf_op jit(solution)/shard_map/ppermute | solution.py:13
  526.4 6.0 collective-permute-done.95
  533.5 11.5 %collective-permute-done.101 = bf16[144,1024]{1,0:T(8,128)(2,1)S(1)} collective-permute-done((bf16[144,1024]{1,0:T(8,128)(2,1)S(1)}, bf16[144,1024]{1,0:T(8,128)(2,1)S(1)}, u32[]{:S(2)}, u32[]{:S(2)}) %collective-permute-start.101) | collective-permute-done | bytes 294944 | tf_op jit(solution)/shard_map/ppermute | solution.py:13
  554.3 16.8 %collective-permute-done.59 = bf16[512,1024]{1,0:T(8,128)(2,1)} collective-permute-done((bf16[512,1024]{1,0:T(8,128)(2,1)S(1)}, bf16[512,1024]{1,0:T(8,128)(2,1)}, u32[]{:S(2)}, u32[]{:S(2)}) %collective-permute-start.59) | collective-permute-done | bytes 1048608 | tf_op jit(solution)/shard_map/ppermute | solution.py:13
  571.2 5.5 bitcast_add_fusion.5
  582.7 8.8 %fusion.31 = (f32[1024]{0:T(1024)S(1)}, f32[512]{0:T(512)S(1)}, bf16[512,1024]{1,0:T(8,128)(2,1)S(1)}, f32[512,1024]{1,0:T(8,128)}) fusion(bf16[2,256,1024]{2,1,0:T(8,128)(2,1)S(1)} %copy-done.13, f32[512]{0:T(512)S(1)} %bitcast.665, f32[1024]{0:T(1024)S(1)} %bitcast.653, bf16[1024,3072]{1,0:T(8,128)(2,1)} %bitcast.50, ...), kind=kOutput, calls=%fused_computation.74 | convolution fusion | flops 3235904000 | bytes 13643776 | tf_op jit(solution)/shard_map/dot_general | solution.py:74
  593.8 5.3 fusion.4
  631.8 9.6 %collective-permute-done.80 = bf16[8,32,1024]{2,1,0:T(8,128)(2,1)S(1)} collective-permute-done((bf16[8,32,1024]{2,1,0:T(8,128)(2,1)S(1)}, bf16[8,32,1024]{2,1,0:T(8,128)(2,1)S(1)}, u32[]{:S(2)}, u32[]{:S(2)}) %collective-permute-start.80) | collective-permute-done | bytes 524320 | tf_op jit(solution)/shard_map/ppermute | solution.py:13
  642.4 6.8 collective-permute-done.81
  656.9 17.8 %collective-permute-done.72 = bf16[8,32,3072]{2,1,0:T(8,128)(2,1)S(1)} collective-permute-done((bf16[8,32,3072]{2,1,0:T(8,128)(2,1)S(1)}, bf16[8,32,3072]{2,1,0:T(8,128)(2,1)S(1)}, u32[]{:S(2)}, u32[]{:S(2)}) %collective-permute-start.72) | collective-permute-done | bytes 1572896 | tf_op jit(solution)/shard_map/ppermute | solution.py:13
  699.1 18.8 %collective-permute-done.74 = bf16[2,32,3072]{2,1,0:T(8,128)(2,1)S(1)} collective-permute-done((bf16[2,32,3072]{2,1,0:T(8,128)(2,1)S(1)}, bf16[2,32,3072]{2,1,0:T(8,128)(2,1)S(1)}, u32[]{:S(2)}, u32[]{:S(2)}) %collective-permute-start.74) | collective-permute-done | bytes 393248 | tf_op jit(solution)/shard_map/ppermute | solution.py:13
  718.1 6.8 collective-permute-done.75
  726.4 6.1 collective-permute-done.77
  (626 shorter events, 395.6 us)
Async XLA Ops:
  2.3 28.5 %collective-permute-start = (bf16[8,128]{1,0:T(8,128)(2,1)}, bf16[8,128]{1,0:T(8,128)(2,1)}, u32[]{:S(2)}, u32[]{:S(2)}) collective-permute-start(bf16[8,128]{1,0:T(8,128)(2,1)} %get-tuple-element.59), channel_id=1, source_target_pairs={{0,2},{1,3},{2,0},{3,1},{4,6},{5,7},{6,4},{7,5},{8,10},{9,11},{10,... | collective-permute-start | bytes 6152 | tf_op jit(solution)/shard_map/ppermute | solution.py:13
  5.3 26.4 %collective-permute-start.1 = (bf16[8,128]{1,0:T(8,128)(2,1)}, bf16[8,128]{1,0:T(8,128)(2,1)}, u32[]{:S(2)}, u32[]{:S(2)}) collective-permute-start(bf16[8,128]{1,0:T(8,128)(2,1)} %get-tuple-element.59), channel_id=1, source_target_pairs={{0,4},{1,5},{2,6},{3,7},{4,0},{5,1},{6,2},{7,3},{8,12},{9,13},{10,... | collective-permute-start | bytes 6152 | tf_op jit(solution)/shard_map/ppermute | solution.py:13
  7.9 30.2 %collective-permute-start.3 = (bf16[8,128]{1,0:T(8,128)(2,1)}, bf16[8,128]{1,0:T(8,128)(2,1)}, u32[]{:S(2)}, u32[]{:S(2)}) collective-permute-start(bf16[8,128]{1,0:T(8,128)(2,1)} %get-tuple-element.59), channel_id=1, source_target_pairs={{0,1},{1,0},{2,3},{3,2},{4,5},{5,4},{6,7},{7,6},{8,9},{9,8},{10,11... | collective-permute-start | bytes 6152 | tf_op jit(solution)/shard_map/ppermute | solution.py:13
  11.0 33.8 %collective-permute-start.7 = (bf16[32,3072]{1,0:T(8,128)(2,1)}, bf16[32,3072]{1,0:T(8,128)(2,1)}, u32[]{:S(2)}, u32[]{:S(2)}) collective-permute-start(bf16[32,3072]{1,0:T(8,128)(2,1)} %constant_dynamic-slice_fusion.14), channel_id=1, source_target_pairs={{0,2},{1,3},{2,0},{3,1},{4,6},{5,7},{6,4},{7,5},{8,10},{9,11},{10,... | collective-permute-start | bytes 589832 | tf_op jit(solution)/shard_map/ppermute | solution.py:13
  11.5 39.4 %collective-permute-start.8 = (bf16[32,3072]{1,0:T(8,128)(2,1)}, bf16[32,3072]{1,0:T(8,128)(2,1)}, u32[]{:S(2)}, u32[]{:S(2)}) collective-permute-start(bf16[32,3072]{1,0:T(8,128)(2,1)} %constant_dynamic-slice_fusion.14), channel_id=1, source_target_pairs={{0,4},{1,5},{2,6},{3,7},{4,0},{5,1},{6,2},{7,3},{8,12},{9,13},{10,... | collective-permute-start | bytes 589832 | tf_op jit(solution)/shard_map/ppermute | solution.py:13
  49.4 26.6 %collective-permute-start.26 = (bf16[32,1024]{1,0:T(8,128)(2,1)S(1)}, bf16[32,1024]{1,0:T(8,128)(2,1)S(1)}, u32[]{:S(2)}, u32[]{:S(2)}) collective-permute-start(bf16[32,1024]{1,0:T(8,128)(2,1)S(1)} %copy-done.71), channel_id=1, source_target_pairs={{0,1},{1,0},{2,3},{3,2},{4,5},{5,4},{6,7},{7,6},{8,9},{9,8},{10,11... | collective-permute-start | bytes 196616 | tf_op jit(solution)/shard_map/ppermute | solution.py:13
  75.9 141.7 %collective-permute-start.62 = (bf16[512,1024]{1,0:T(8,128)(2,1)S(1)}, bf16[512,1024]{1,0:T(8,128)(2,1)}, u32[]{:S(2)}, u32[]{:S(2)}) collective-permute-start(bf16[512,1024]{1,0:T(8,128)(2,1)S(1)} %copy-done.24), channel_id=1, source_target_pairs={{0,16},{8,24},{16,0},{24,8},{1,17},{9,25},{17,1},{25,9},{2,18},{10... | collective-permute-start | bytes 3145736 | tf_op jit(solution)/shard_map/ppermute | solution.py:13
  80.4 140.2 %collective-permute-start.60 = (bf16[512,1024]{1,0:T(8,128)(2,1)S(1)}, bf16[512,1024]{1,0:T(8,128)(2,1)}, u32[]{:S(2)}, u32[]{:S(2)}) collective-permute-start(bf16[512,1024]{1,0:T(8,128)(2,1)S(1)} %copy-done.24), channel_id=1, source_target_pairs={{0,8},{8,0},{16,24},{24,16},{1,9},{9,1},{17,25},{25,17},{2,10},{10... | collective-permute-start | bytes 3145736 | tf_op jit(solution)/shard_map/ppermute | solution.py:13
  113.7 46.7 %collective-permute-start.42 = (bf16[128,1152]{1,0:T(8,128)(2,1)S(1)}, bf16[128,1152]{1,0:T(8,128)(2,1)}, u32[]{:S(2)}, u32[]{:S(2)}) collective-permute-start(bf16[128,1152]{1,0:T(8,128)(2,1)S(1)} %copy.45), channel_id=1, source_target_pairs={{0,4},{1,5},{2,6},{3,7},{4,0},{5,1},{6,2},{7,3},{8,12},{9,13},{10,... | collective-permute-start | bytes 884744 | tf_op jit(solution)/shard_map/ppermute | solution.py:13
  168.1 33.3 %collective-permute-start.48 = (bf16[144,1024]{1,0:T(8,128)(2,1)S(1)}, bf16[144,1024]{1,0:T(8,128)(2,1)S(1)}, u32[]{:S(2)}, u32[]{:S(2)}) collective-permute-start(bf16[144,1024]{1,0:T(8,128)(2,1)S(1)} %copy-done.37), channel_id=1, source_target_pairs={{0,2},{1,3},{2,0},{3,1},{4,6},{5,7},{6,4},{7,5},{8,10},{9,11},{10,... | collective-permute-start | bytes 884744 | tf_op jit(solution)/shard_map/ppermute | solution.py:13
  208.9 49.7 %collective-permute-start.17 = (bf16[4,32,3072]{2,1,0:T(8,128)(2,1)}, bf16[4,32,3072]{2,1,0:T(8,128)(2,1)}, u32[]{:S(2)}, u32[]{:S(2)}) collective-permute-start(bf16[4,32,3072]{2,1,0:T(8,128)(2,1)} %pad_maximum_fusion.4), channel_id=1, source_target_pairs={{0,8},{8,0},{16,24},{24,16},{1,9},{9,1},{17,25},{25,17},{2,10},{10... | collective-permute-start | bytes 2359304 | tf_op jit(solution)/shard_map/ppermute | solution.py:13
  209.2 32.2 %collective-permute-start.18 = (bf16[4,32,3072]{2,1,0:T(8,128)(2,1)}, bf16[4,32,3072]{2,1,0:T(8,128)(2,1)S(1)}, u32[]{:S(2)}, u32[]{:S(2)}) collective-permute-start(bf16[4,32,3072]{2,1,0:T(8,128)(2,1)} %pad_maximum_fusion.4), channel_id=1, source_target_pairs={{0,16},{8,24},{16,0},{24,8},{1,17},{9,25},{17,1},{25,9},{2,18},{10... | collective-permute-start | bytes 2359304 | tf_op jit(solution)/shard_map/ppermute | solution.py:13
  220.6 31.3 %collective-permute-start.12 = (bf16[3,32,3072]{2,1,0:T(8,128)(2,1)}, bf16[3,32,3072]{2,1,0:T(8,128)(2,1)S(1)}, u32[]{:S(2)}, u32[]{:S(2)}) collective-permute-start(bf16[3,32,3072]{2,1,0:T(8,128)(2,1)} %collective-permute-done.11), channel_id=1, source_target_pairs={{0,8},{8,0},{16,24},{24,16},{1,9},{9,1},{17,25},{25,17},{2,10},{10... | collective-permute-start | bytes 1769480 | tf_op jit(solution)/shard_map/ppermute | solution.py:13
  241.3 50.0 %collective-permute-start.63 = (bf16[512,1024]{1,0:T(8,128)(2,1)}, bf16[512,1024]{1,0:T(8,128)(2,1)S(1)}, u32[]{:S(2)}, u32[]{:S(2)}) collective-permute-start(bf16[512,1024]{1,0:T(8,128)(2,1)} %collective-permute-done.62), channel_id=1, source_target_pairs={{0,8},{8,0},{16,24},{24,16},{1,9},{9,1},{17,25},{25,17},{2,10},{10... | collective-permute-start | bytes 3145736 | tf_op jit(solution)/shard_map/ppermute | solution.py:13
  290.8 48.6 %collective-permute-start.56 = (bf16[512,1024]{1,0:T(8,128)(2,1)S(1)}, bf16[512,1024]{1,0:T(8,128)(2,1)S(1)}, u32[]{:S(2)}, u32[]{:S(2)}) collective-permute-start(bf16[512,1024]{1,0:T(8,128)(2,1)S(1)} %multiply_convert_fusion.6), channel_id=1, source_target_pairs={{0,16},{8,24},{16,0},{24,8},{1,17},{9,25},{17,1},{25,9},{2,18},{10... | collective-permute-start | bytes 3145736 | tf_op jit(solution)/shard_map/ppermute | solution.py:13
  331.6 217.6 %collective-permute-start.61 = (bf16[512,1024]{1,0:T(8,128)(2,1)}, bf16[512,1024]{1,0:T(8,128)(2,1)}, u32[]{:S(2)}, u32[]{:S(2)}) collective-permute-start(bf16[512,1024]{1,0:T(8,128)(2,1)} %slice.509), channel_id=1, source_target_pairs={{0,8},{8,0},{16,24},{24,16},{1,9},{9,1},{17,25},{25,17},{2,10},{10... | collective-permute-start | bytes 3145736 | tf_op jit(solution)/shard_map/ppermute | solution.py:13
  339.2 213.9 %collective-permute-start.55 = (bf16[512,1024]{1,0:T(8,128)(2,1)}, bf16[512,1024]{1,0:T(8,128)(2,1)}, u32[]{:S(2)}, u32[]{:S(2)}) collective-permute-start(bf16[512,1024]{1,0:T(8,128)(2,1)} %slice.511), channel_id=1, source_target_pairs={{0,8},{8,0},{16,24},{24,16},{1,9},{9,1},{17,25},{25,17},{2,10},{10... | collective-permute-start | bytes 3145736 | tf_op jit(solution)/shard_map/ppermute | solution.py:13
  376.2 44.5 %collective-permute-start.64 = (bf16[512,1024]{1,0:T(8,128)(2,1)}, bf16[512,1024]{1,0:T(8,128)(2,1)}, u32[]{:S(2)}, u32[]{:S(2)}) collective-permute-start(bf16[512,1024]{1,0:T(8,128)(2,1)} %slice.508), channel_id=1, source_target_pairs={{0,8},{8,0},{16,24},{24,16},{1,9},{9,1},{17,25},{25,17},{2,10},{10... | collective-permute-start | bytes 3145736 | tf_op jit(solution)/shard_map/ppermute | solution.py:13
  383.4 41.9 %collective-permute-start.58 = (bf16[512,1024]{1,0:T(8,128)(2,1)}, bf16[512,1024]{1,0:T(8,128)(2,1)}, u32[]{:S(2)}, u32[]{:S(2)}) collective-permute-start(bf16[512,1024]{1,0:T(8,128)(2,1)} %slice.510), channel_id=1, source_target_pairs={{0,8},{8,0},{16,24},{24,16},{1,9},{9,1},{17,25},{25,17},{2,10},{10... | collective-permute-start | bytes 3145736 | tf_op jit(solution)/shard_map/ppermute | solution.py:13
  392.5 35.4 %collective-permute-start.93 = (bf16[2,2,128,1152]{2,3,1,0:T(8,128)(2,1)}, bf16[2,2,128,1152]{2,3,1,0:T(8,128)(2,1)}, u32[]{:S(2)}, u32[]{:S(2)}) collective-permute-start(bf16[2,2,128,1152]{2,3,1,0:T(8,128)(2,1)} %bitcast.623), channel_id=1, source_target_pairs={{0,1},{1,0},{2,3},{3,2},{4,5},{5,4},{6,7},{7,6},{8,9},{9,8},{10,11... | collective-permute-start | bytes 3538952 | tf_op jit(solution)/shard_map/ppermute | solution.py:13
  420.8 29.4 %collective-permute-start.87 = (bf16[2,2,128,1152]{2,3,1,0:T(8,128)(2,1)}, bf16[2,2,128,1152]{2,3,1,0:T(8,128)(2,1)S(1)}, u32[]{:S(2)}, u32[]{:S(2)}) collective-permute-start(bf16[2,2,128,1152]{2,3,1,0:T(8,128)(2,1)} %bitcast.624), channel_id=1, source_target_pairs={{0,1},{1,0},{2,3},{3,2},{4,5},{5,4},{6,7},{7,6},{8,9},{9,8},{10,11... | collective-permute-start | bytes 3538952 | tf_op jit(solution)/shard_map/ppermute | solution.py:13
  425.4 49.3 %collective-permute-start.99 = (bf16[2,2,144,1024]{3,2,1,0:T(8,128)(2,1)S(1)}, bf16[2,2,144,1024]{3,2,1,0:T(8,128)(2,1)S(1)}, u32[]{:S(2)}, u32[]{:S(2)}) collective-permute-start(bf16[2,2,144,1024]{3,2,1,0:T(8,128)(2,1)S(1)} %fusion.34), channel_id=1, source_target_pairs={{0,1},{1,0},{2,3},{3,2},{4,5},{5,4},{6,7},{7,6},{8,9},{9,8},{10,11... | collective-permute-start | bytes 3538952 | tf_op jit(solution)/shard_map/ppermute | solution.py:13
  427.9 121.4 %collective-permute-start.65 = (bf16[512,1024]{1,0:T(8,128)(2,1)S(1)}, bf16[512,1024]{1,0:T(8,128)(2,1)S(1)}, u32[]{:S(2)}, u32[]{:S(2)}) collective-permute-start(bf16[512,1024]{1,0:T(8,128)(2,1)S(1)} %fusion.9), channel_id=1, source_target_pairs={{0,16},{8,24},{16,0},{24,8},{1,17},{9,25},{17,1},{25,9},{2,18},{10... | collective-permute-start | bytes 3145736 | tf_op jit(solution)/shard_map/ppermute | solution.py:13
  474.7 38.8 %collective-permute-start.88 = (bf16[2,128,1152]{1,2,0:T(8,128)(2,1)S(1)}, bf16[2,128,1152]{1,2,0:T(8,128)(2,1)S(1)}, u32[]{:S(2)}, u32[]{:S(2)}) collective-permute-start(bf16[2,128,1152]{1,2,0:T(8,128)(2,1)S(1)} %dynamic-slice_bitcast_fusion.3), channel_id=1, source_target_pairs={{0,4},{1,5},{2,6},{3,7},{4,0},{5,1},{6,2},{7,3},{8,12},{9,13},{10,... | collective-permute-start | bytes 1769480 | tf_op jit(solution)/shard_map/ppermute | solution.py:13
  475.5 50.7 %collective-permute-start.100 = (bf16[2,144,1024]{2,1,0:T(8,128)(2,1)S(1)}, bf16[2,144,1024]{2,1,0:T(8,128)(2,1)S(1)}, u32[]{:S(2)}, u32[]{:S(2)}) collective-permute-start(bf16[2,144,1024]{2,1,0:T(8,128)(2,1)S(1)} %dynamic-slice_bitcast_fusion.1), channel_id=1, source_target_pairs={{0,4},{1,5},{2,6},{3,7},{4,0},{5,1},{6,2},{7,3},{8,12},{9,13},{10,... | collective-permute-start | bytes 1769480 | tf_op jit(solution)/shard_map/ppermute | solution.py:13
  545.0 26.2 %collective-permute-start.59 = (bf16[512,1024]{1,0:T(8,128)(2,1)S(1)}, bf16[512,1024]{1,0:T(8,128)(2,1)}, u32[]{:S(2)}, u32[]{:S(2)}) collective-permute-start(bf16[512,1024]{1,0:T(8,128)(2,1)S(1)} %fusion.11), channel_id=1, source_target_pairs={{0,16},{8,24},{16,0},{24,8},{1,17},{9,25},{17,1},{25,9},{2,18},{10... | collective-permute-start | bytes 3145736 | tf_op jit(solution)/shard_map/ppermute | solution.py:13
  548.1 66.0 %collective-permute-start.96 = (bf16[128,1152]{0,1:T(8,128)(2,1)}, bf16[128,1152]{0,1:T(8,128)(2,1)}, u32[]{:S(2)}, u32[]{:S(2)}) collective-permute-start(bf16[128,1152]{0,1:T(8,128)(2,1)} %get-tuple-element.49), channel_id=1, source_target_pairs={{0,8},{8,0},{16,24},{24,16},{1,9},{9,1},{17,25},{25,17},{2,10},{10... | collective-permute-start | bytes 884744 | tf_op jit(solution)/shard_map/ppermute | solution.py:13
  549.2 66.4 %collective-permute-start.97 = (bf16[128,1152]{0,1:T(8,128)(2,1)}, bf16[128,1152]{0,1:T(8,128)(2,1)S(1)}, u32[]{:S(2)}, u32[]{:S(2)}) collective-permute-start(bf16[128,1152]{0,1:T(8,128)(2,1)} %get-tuple-element.49), channel_id=1, source_target_pairs={{0,16},{8,24},{16,0},{24,8},{1,17},{9,25},{17,1},{25,9},{2,18},{10... | collective-permute-start | bytes 884744 | tf_op jit(solution)/shard_map/ppermute | solution.py:13
  550.2 67.5 %collective-permute-start.90 = (bf16[128,1152]{0,1:T(8,128)(2,1)}, bf16[128,1152]{0,1:T(8,128)(2,1)}, u32[]{:S(2)}, u32[]{:S(2)}) collective-permute-start(bf16[128,1152]{0,1:T(8,128)(2,1)} %get-tuple-element.51), channel_id=1, source_target_pairs={{0,8},{8,0},{16,24},{24,16},{1,9},{9,1},{17,25},{25,17},{2,10},{10... | collective-permute-start | bytes 884744 | tf_op jit(solution)/shard_map/ppermute | solution.py:13
  553.1 65.8 %collective-permute-start.91 = (bf16[128,1152]{0,1:T(8,128)(2,1)}, bf16[128,1152]{0,1:T(8,128)(2,1)}, u32[]{:S(2)}, u32[]{:S(2)}) collective-permute-start(bf16[128,1152]{0,1:T(8,128)(2,1)} %get-tuple-element.51), channel_id=1, source_target_pairs={{0,16},{8,24},{16,0},{24,8},{1,17},{9,25},{17,1},{25,9},{2,18},{10... | collective-permute-start | bytes 884744 | tf_op jit(solution)/shard_map/ppermute | solution.py:13
  625.0 52.1 %collective-permute-start.104 = (bf16[144,1024]{1,0:T(8,128)(2,1)}, bf16[144,1024]{1,0:T(8,128)(2,1)}, u32[]{:S(2)}, u32[]{:S(2)}) collective-permute-start(bf16[144,1024]{1,0:T(8,128)(2,1)} %collective-permute-done.103), channel_id=1, source_target_pairs={{0,8},{8,0},{16,24},{24,16},{1,9},{9,1},{17,25},{25,17},{2,10},{10... | collective-permute-start | bytes 884744 | tf_op jit(solution)/shard_map/ppermute | solution.py:13
  631.4 43.3 %collective-permute-start.72 = (bf16[8,32,3072]{2,1,0:T(8,128)(2,1)S(1)}, bf16[8,32,3072]{2,1,0:T(8,128)(2,1)S(1)}, u32[]{:S(2)}, u32[]{:S(2)}) collective-permute-start(bf16[8,32,3072]{2,1,0:T(8,128)(2,1)S(1)} %dynamic-slice_bitcast_fusion), channel_id=1, source_target_pairs={{0,16},{8,24},{16,0},{24,8},{1,17},{9,25},{17,1},{25,9},{2,18},{10... | collective-permute-start | bytes 4718600 | tf_op jit(solution)/shard_map/ppermute | solution.py:13
  (163 other events, 1932.0 us)

commit v2 on v1

--- a/solution.py
+++ b/solution.py
@@ -1,11 +1,16 @@
+import functools
+
 import jax
 import jax.numpy as jnp
 from jax import lax
+from jax.experimental import pallas as pl
+from jax.experimental.pallas import tpu as pltpu
 from jax.sharding import PartitionSpec as P
 
 EPSILON = 1e-05
 LOW = jnp.bfloat16
 F32 = jnp.float32
+MESH = pl.DeviceIdType.MESH
 
 
 def hop(values, axis, bit):
@@ -151,6 +156,323 @@
     return share_quarters(own).reshape(4 * quarter, cols).astype(F32)
 
 
+def flipped(index, offset):
+    bit = 1
+    while bit <= offset:
+        if offset & bit:
+            index = index + bit - 2 * bit * ((index // bit) % 2)
+        bit *= 2
+    return index
+
+
+class Copies:
+    def __init__(self, send_sems, recv_sems):
+        self.sems = send_sems, recv_sems
+        self.rep = lax.axis_index("rep")
+        self.place = lax.axis_index("fsdp")
+        self.started = []
+
+    def peer(self, rep_bits, place_bits):
+        return (flipped(self.rep, rep_bits), flipped(self.place, place_bits))
+
+    def meet(self, peers):
+        barrier = pltpu.get_barrier_semaphore()
+        for bits in peers:
+            pl.semaphore_signal(barrier, inc=1, device_id=self.peer(*bits), device_id_type=MESH)
+        pl.semaphore_wait(barrier, len(peers))
+
+    def send(self, source, target, rep_bits, place_bits):
+        at = len(self.started)
+        copy = pltpu.make_async_remote_copy(
+            src_ref=source,
+            dst_ref=target,
+            send_sem=self.sems[0].at[at],
+            recv_sem=self.sems[1].at[at],
+            device_id=self.peer(rep_bits, place_bits),
+            device_id_type=MESH,
+        )
+        copy.start()
+        self.started.append(copy)
+        return copy
+
+    def close(self):
+        for copy in self.started:
+            copy.wait_send()
+
+
+class Local:
+    def __init__(self, sems):
+        self.sems = sems
+        self.started = []
+
+    def copy(self, source, target):
+        copy = pltpu.make_async_copy(source, target, self.sems.at[len(self.started)])
+        copy.start()
+        self.started.append(copy)
+        return copy
+
+
+class Spread:
+    def __init__(self, copies, locals_, shards, source, target, at=None):
+        self.copies = copies
+        self.target = target
+        self.at = at if at is not None else (lambda shard: target.at[shard])
+        self.source = source
+        self.locals = locals_
+        self.far = list(range(2, shards, 2))
+        self.near = [1] + [offset + 1 for offset in self.far]
+
+    def start(self):
+        copies = self.copies
+        here = self.at(copies.place)
+        self.arriving = {offset: copies.send(self.source, here, 0, offset) for offset in self.far}
+        self.arriving[1] = copies.send(self.source, here, 0, 1)
+        if self.locals is not None:
+            self.own = self.locals.copy(self.source, here)
+
+    def arrive(self, offset):
+        self.arriving[offset].wait_recv()
+        if offset % 2 == 0:
+            block = self.at(flipped(self.copies.place, offset))
+            self.arriving[offset + 1] = self.copies.send(block, block, 0, 1)
+
+    def finish(self):
+        for offset in self.near:
+            self.arriving[offset].wait_recv()
+        if self.locals is not None:
+            self.own.wait()
+
+
+class SpreadAll(Spread):
+    def __init__(self, copies, locals_, shards, source, target, width):
+        self.width = width
+        self.whole = source
+        self.local_all = locals_
+        rep = copies.rep
+        super().__init__(
+            copies,
+            None,
+            shards,
+            source.at[:, self.columns(rep)],
+            target,
+            lambda shard: target.at[shard, :, self.columns(rep)],
+        )
+        self.across = {}
+        self.core = []
+
+    def columns(self, rep):
+        return pl.ds(pl.multiple_of(rep * self.width, self.width), self.width)
+
+    def start(self):
+        super().start()
+        self.own = self.local_all.copy(self.whole, self.target.at[self.copies.place])
+
+    def arrive(self, offset):
+        super().arrive(offset)
+        block = self.at(flipped(self.copies.place, offset))
+        self.across[offset] = self.copies.send(block, block, 2, 0)
+        self.core.append(self.copies.send(block, block, 1, 0))
+
+    def cross(self, offset):
+        copies = self.copies
+        self.across[offset].wait_recv()
+        shard = flipped(copies.place, offset)
+        block = self.target.at[shard, :, self.columns(flipped(copies.rep, 2))]
+        self.core.append(copies.send(block, block, 1, 0))
+
+    def finish(self):
+        for copy in self.core:
+            copy.wait_recv()
+        self.own.wait()
+
+
+def row_loop(rows, step, body):
+    @pl.loop(0, rows // step)
+    def _(at):
+        body(pl.ds(pl.multiple_of(at * step, step), step))
+
+
+def normed(values, gain):
+    return values * rms_scale(values) * gain
+
+
+def shifted(values, by):
+    rows = values.shape[0]
+    at = lax.broadcasted_iota(jnp.int32, values.shape, 0)
+    turned = pltpu.roll(values, by % rows, 0)
+    kept = at >= by if by > 0 else at < rows + by
+    return jnp.where(kept, turned, 0.0)
+
+
+def mixer_columns(act, m_in, gains, at, width, features, slot):
+    lanes = pl.ds(at, width)
+    parts = []
+    for base in (0, features, 2 * features):
+        block = m_in[:, :, base + at : base + at + width].reshape(features, width)
+        parts.append(dot(act, block))
+    part_b, part_c, part_x = parts
+    taps = [gains[2 + k : 3 + k, at : at + width] for k in range(3)]
+    product = part_b * part_x
+    convolved = []
+    for start in range(0, act.shape[0], slot):
+        rows = product[start : start + slot]
+        convolved.append(
+            taps[0] * shifted(rows, 2) + taps[1] * shifted(rows, 1) + taps[2] * rows
+        )
+    return part_b, part_c, part_x, product, jnp.concatenate(convolved)
+
+
+def forward_kernel(
+    slot,
+    rows_ref, cot_ref, small_ref, in_ref, out_ref, gate_ref, up_ref, down_ref,
+    all_in, all_out, all_gate, all_up, all_down, all_act, all_cot, gains_ref,
+    small_all, v_in, v_out, act_one, mixer_in, act_two,
+    send_sems, recv_sems, local_sems,
+):
+    rows, features = rows_ref.shape
+    shards = all_gate.shape[0]
+    copies = Copies(send_sems, recv_sems)
+    local = Local(local_sems)
+    far = list(range(2, shards, 2))
+    copies.meet([(0, offset) for offset in [*far, 1]] + [(1, 0), (2, 0)])
+
+    small = Spread(copies, local, shards, small_ref, small_all)
+    w_in = SpreadAll(copies, local, shards, in_ref, v_in, in_ref.shape[1] // 4)
+    w_out = SpreadAll(copies, local, shards, out_ref, v_out, out_ref.shape[1] // 4)
+    gate = Spread(copies, local, shards, gate_ref, all_gate)
+    up = Spread(copies, local, shards, up_ref, all_up)
+    down = Spread(copies, local, shards, down_ref, all_down)
+
+    small.start()
+    w_in.start()
+    w_out.start()
+    own_cot = local.copy(cot_ref, all_cot.at[0])
+    for offset in far:
+        small.arrive(offset)
+    small.finish()
+    gains_ref[...] = jnp.sum(small_all[...], axis=0)
+    gain_one = gains_ref[0:1]
+
+    def first(at):
+        act_one[at] = normed(rows_ref[at].astype(F32), gain_one).astype(LOW)
+
+    w_in.arrive(far[0])
+    w_in.arrive(1)
+    row_loop(rows, 64, first)
+    gate.start()
+    for offset in far[1:]:
+        w_in.arrive(offset)
+    for offset in far:
+        w_in.arrive(offset + 1)
+    w_out.arrive(1)
+    for offset in far:
+        w_out.arrive(offset)
+    for offset in far:
+        w_out.arrive(offset + 1)
+    up.start()
+    cot_core = copies.send(cot_ref, all_cot.at[1], 1, 0)
+    cot_across = copies.send(cot_ref, all_cot.at[2], 2, 0)
+    order = [1, *far, *[offset + 1 for offset in far]]
+    for offset in order:
+        w_in.cross(offset)
+    for offset in far:
+        gate.arrive(offset)
+    for offset in order:
+        w_out.cross(offset)
+    down.start()
+    w_in.finish()
+
+    width = features // 4
+    for part in range(4):
+        at = part * width
+        _, part_c, _, _, convolved = mixer_columns(
+            act_one[...], v_in, gains_ref, at, width, features, slot
+        )
+        mixer_in[:, at : at + width] = (part_c * convolved).astype(LOW)
+        if part == 1:
+            for offset in far:
+                up.arrive(offset)
+    keep_in = local.copy(v_in, all_in)
+    w_out.finish()
+    keep_out = local.copy(v_out, all_out)
+    spread = []
+    for start in range(0, rows, slot):
+        held = slice(start, start + slot)
+        hstate = rows_ref[held].astype(F32) + dot(
+            mixer_in[held], v_out[...].reshape(features, features)
+        )
+        act_two[held] = normed(hstate, gains_ref[1:2]).astype(LOW)
+        block = act_two.at[held]
+        spread.append(
+            (
+                held,
+                copies.send(block, all_act.at[2, held], 2, 0),
+                copies.send(block, all_act.at[1, held], 1, 0),
+                local.copy(block, all_act.at[0, held]),
+            )
+        )
+    for offset in far:
+        down.arrive(offset)
+    cot_across.wait_recv()
+    corner = [copies.send(all_cot.at[2], all_cot.at[3], 1, 0)]
+    for held, across, _, _ in spread:
+        across.wait_recv()
+        corner.append(copies.send(all_act.at[2, held], all_act.at[3, held], 1, 0))
+    gate.finish()
+    up.finish()
+    down.finish()
+    cot_core.wait_recv()
+    for _, _, core, own in spread:
+        core.wait_recv()
+        own.wait()
+    for copy in corner:
+        copy.wait_recv()
+    own_cot.wait()
+    keep_in.wait()
+    keep_out.wait()
+    copies.close()
+
+
+def run_forward(rows, cot, small, w_in, w_out, gate, up, down, slot):
+    shards = lax.axis_size("fsdp")
+    count, features = rows.shape
+    part = w_in.shape[0]
+    shapes = [
+        ((shards, *w_in.shape), LOW),
+        ((shards, *w_out.shape), LOW),
+        ((shards, *gate.shape), LOW),
+        ((shards, *up.shape), LOW),
+        ((shards, *down.shape), LOW),
+        ((4, count, features), LOW),
+        ((4, count, features), LOW),
+    ]
+    hbm = pl.BlockSpec(memory_space=pltpu.HBM)
+    vmem = pl.BlockSpec(memory_space=pltpu.VMEM)
+    hops = 12 * shards + 16
+    return pl.pallas_call(
+        functools.partial(forward_kernel, slot),
+        out_shape=[jax.ShapeDtypeStruct(*shape) for shape in shapes]
+        + [jax.ShapeDtypeStruct((8, features), F32)],
+        in_specs=[vmem, hbm, vmem, hbm, hbm, hbm, hbm, hbm],
+        out_specs=[hbm] * 7 + [vmem],
+        scratch_shapes=[
+            pltpu.VMEM((shards, 8, features), F32),
+            pltpu.VMEM((shards, *w_in.shape), LOW),
+            pltpu.VMEM((shards, *w_out.shape), LOW),
+            pltpu.VMEM((count, features), LOW),
+            pltpu.VMEM((count, features), LOW),
+            pltpu.VMEM((count, features), LOW),
+            pltpu.SemaphoreType.DMA((hops,)),
+            pltpu.SemaphoreType.DMA((hops,)),
+            pltpu.SemaphoreType.DMA((16,)),
+        ],
+        compiler_params=pltpu.CompilerParams(
+            collective_id=0, has_side_effects=True, vmem_limit_bytes=56 << 20
+        ),
+        name="forward",
+    )(rows, cot, small, w_in, w_out, gate, up, down)
+
+
 def on_device(
     inputs, cotangent, lengths, norm_one, w_in, conv_w, w_out, norm_two, w_gate, w_up, w_down
 ):
@@ -163,13 +485,18 @@
     cut = hidden_own // 4
     part_ff = shards * cut
 
+    slot_cols = jnp.arange(lengths.shape[1], dtype=jnp.int32)
+    slot_id = rep * shards + place
+    length_now = jnp.sum(jnp.where(slot_cols == slot_id, lengths, 0), axis=1)
+    position = jnp.arange(tok_rows, dtype=jnp.int32)
+    live = (position[None] < length_now[:, None]).astype(F32)[..., None]
+    cotan_f = (cotangent.astype(F32) * live).reshape(all_rows, features)
+    cotan_low = cotan_f.astype(LOW)
+
     small = jnp.concatenate([norm_one[None], norm_two[None], conv_w, jnp.zeros_like(conv_w)])
-    small_all = in_order(gather_pieces(small), place)
-    small_all = jnp.moveaxis(small_all, 0, 1).reshape(8, features).astype(F32)
-    g_one, g_two, taps = small_all[0], small_all[1], small_all[2:5]
-
-    m_in, in_pieces = gather_full(w_in)
-    m_out, out_pieces = gather_full(w_out, in_pieces[2])
+    small = lax.dynamic_update_slice(
+        jnp.zeros((8, features), F32), small.astype(F32), (0, place * small.shape[1])
+    )
     gate_own = lax.dynamic_index_in_dim(
         w_gate.reshape(-1, shards, 4, cut), rep, 2, keepdims=False
     ).reshape(-1, part_ff)
@@ -177,21 +504,18 @@
         w_up.reshape(-1, shards, 4, cut), rep, 2, keepdims=False
     ).reshape(-1, part_ff)
     down_own = lax.dynamic_slice_in_dim(w_down, rep * cut, cut, 0)
-    gate_pieces = gather_pieces(after(gate_own, in_pieces[4]))
-    up_pieces = gather_pieces(after(up_own, gate_pieces[4]))
-    down_pieces = gather_pieces(after(down_own, up_pieces[4]))
-    m_gate = in_order(gate_pieces, place).reshape(features, part_ff)
-    m_up = in_order(up_pieces, place).reshape(features, part_ff)
-    m_down = in_order(down_pieces, place).reshape(part_ff, features)
-
-    slot_cols = jnp.arange(lengths.shape[1], dtype=jnp.int32)
-    slot_id = rep * shards + place
-    length_now = jnp.sum(jnp.where(slot_cols == slot_id, lengths, 0), axis=1)
-    position = jnp.arange(tok_rows, dtype=jnp.int32)
-    live = (position[None] < length_now[:, None]).astype(F32)[..., None]
-    cotan_f = (cotangent.astype(F32) * live).reshape(all_rows, features)
-    cotan_low = cotan_f.astype(LOW)
-    cot_near, cot_far = spread_over_rep(after(cotan_low, in_pieces[1]))
+    rows_low = inputs.reshape(all_rows, features)
+    m_in, m_out, m_gate, m_up, m_down, act_all, cot_all, gains = run_forward(
+        rows_low, cotan_low, small, w_in, w_out, gate_own, up_own, down_own, tok_rows
+    )
+    m_in = m_in.reshape(features, -1)
+    m_out = m_out.reshape(features, -1)
+    m_gate = m_gate.reshape(features, part_ff)
+    m_up = m_up.reshape(features, part_ff)
+    m_down = m_down.reshape(part_ff, features)
+    g_one, g_two, taps = gains[0], gains[1], gains[2:5]
+    act_near, act_far = act_all[:2].reshape(-1, features), act_all[2:].reshape(-1, features)
+    cot_near, cot_far = cot_all[:2].reshape(-1, features), cot_all[2:].reshape(-1, features)
 
     rows_f = inputs.reshape(all_rows, features).astype(F32)
     scale_one = rms_scale(rows_f)
@@ -209,7 +533,6 @@
     hstate = rows_f + dot(mixer_in, m_out)
     scale_two = rms_scale(hstate)
     act_two = (hstate * scale_two * g_two).astype(LOW)
-    act_near, act_far = spread_over_rep(act_two)
 
     def units(act, cot):
         gate_pre = dot(act, m_gate)

time: 747 us -> 587 us (0.79)
  Pallas kernels: 0 us -> 126 us
  waiting for transfers between devices: 302 us -> 193 us
  local copies, waits for them, and re-layouts: 166 us -> 75.4 us
  starting transfers between devices: 87.9 us -> 28.8 us
  matrix products: 130 us -> 113 us
    pallas_call x0 -> x1, Pallas kernels: none -> 126 us  [run_forward(): pl.pallas_call(functools.partial(forward_kernel, slot), out_shape=[jax.Sh...]
    ppermute x105 -> x45, waiting for transfers between devices: 302 us -> 193 us  [hop(): return lax.ppermute(values, axis, [(at, at ^ bit) for at in range(size)])]
    dynamic_update_slice x103 -> x15, local copies, waits for them, and re-layouts: 83.1 us -> 3.28 us  [put(): lax.dynamic_update_slice(target, block, index + (0,) * (target.ndim - len...]
    ppermute x105 -> x45, starting transfers between devices: 87.9 us -> 28.8 us  [hop(): return lax.ppermute(values, axis, [(at, at ^ bit) for at in range(size)])]
    broadcast_in_dim x12 -> x1, local copies, waits for them, and re-layouts: 14.9 us -> 0.01 us  [on_device(): jnp.zeros((8, features), F32)]
    dot_general x8, matrix products: 54 us -> 41.9 us  [dot(): return jnp.dot(left, right, preferred_element_type=F32)]
    unnamed x190 -> x151, local copies, waits for them, and re-layouts: 28.9 us -> 30.2 us
  transfers between devices with their start and end apart: 105 -> 45, of which waited for: 42 -> 18; matrix products, arithmetic and copies ran while one was open for 45% -> 24% of each run, Pallas kernels for 0% -> 0%
where the time goes in v2:
time: 587 us; the launch traced here: 578 us
  waiting for transfers between devices  193 us (33%)
  Pallas kernels  126 us (21%)
  matrix products  113 us (19%)
  local copies, waits for them, and re-layouts  75.4 us (13%)
  other arithmetic  39.6 us (7%)
  starting transfers between devices  28.8 us (5%)
    ppermute x45, waiting for transfers between devices, hop(): return lax.ppermute(values, axis, [(at, at ^ bit) for at in range(size)])  193 us
    pallas_call x1, Pallas kernels, run_forward(): pl.pallas_call(functools.partial(forward_kernel, slot), out_shape=[jax.Sh...  126 us
    dot_general x8, matrix products, dot(): return jnp.dot(left, right, preferred_element_type=F32)  41.9 us
    dot_general x8, matrix products, dot_last(): lax.dot_general(left, right, (((1,), (1,)), ((), ())), preferred_element_...  39.8 us
    dot_general x8, matrix products, dot_first(): lax.dot_general(left, right, (((0,), (0,)), ((), ())), preferred_element_...  31.6 us
    unnamed x151, local copies, waits for them, and re-layouts  30.2 us
    ppermute x45, starting transfers between devices, hop(): return lax.ppermute(values, axis, [(at, at ^ bit) for at in range(size)])  28.8 us
  transfers between devices with their start and end apart: 45, of which 18 were waited for; matrix products, arithmetic and copies ran while one was open for 24% of the time, Pallas kernels for 0%

profile of v2, /device:TPU:0, one launch (start us, length us, event | category | flops | bytes accessed | tf_op | source)
XLA Modules:
  0.0 577.7 jit_solution(15389603575084242030)
XLA Ops:
  14.3 125.7 %forward.1 = (bf16[8,128,3072]{2,1,0:T(8,128)(2,1)}, bf16[8,128,1024]{2,1,0:T(8,128)(2,1)}, bf16[8,128,1152]{2,1,0:T(8,128)(2,1)}, bf16[8,128,1152]{2,1,0:T(8,12...) custom-call(bf16[512,1024]{1,0:T(8,128)(2,1)} %bitcast.319, ...), custom_call_target="tpu_custom_call" | custom-call | tf_op jit(solution)/shard_map/forward/pallas_call | solution.py:452
  148.8 16.3 %fusion.79 = f32[1024,1152]{1,0:T(8,128)} fusion(bf16[1024,1024]{1,0:T(8,128)(2,1)S(1)} %bitcast.342, bf16[1024,1152]{1,0:T(8,128)(2,1)S(1)} %bitcast.391), kind=kOutput, calls=%fused_computation.207 | convolution fusion | flops 2415919104 | bytes 9175040 | tf_op jit(solution)/shard_map/dot_general | solution.py:75
  165.1 4.5 fusion.78
  171.8 5.9 %multiply_convert_fusion.2 = (bf16[1024,1152]{1,0:T(8,128)(2,1)}, bf16[1024,1152]{1,0:T(8,128)(2,1)}, bf16[1024,1152]{1,0:T(8,128)(2,1)S(1)}) fusion(f32[1024,1152]{1,0:T(8,128)S(1)} %fusion.75, f32[1024,1152]{1,0:T(8,128)S(1)} %fusion.76, bf16[1024,1024]{1,0:T(8,128)(2,1)S(1)} %bitcast.352, bf16[1152,1024]{1,0:T(8,128)(2,1)S(1)} %bitcast.399), kind=kOutput, calls=%fused_computation.5 | convolution fusion | flops 2433613824 | bytes 20971520 | tf_op jit(solution)/shard_map/dot_general | solution.py:79
  179.2 4.4 fusion.85
  183.6 11.6 %multiply_convert_fusion = (bf16[1024,1152]{1,0:T(8,128)(2,1)}, bf16[1024,1152]{1,0:T(8,128)(2,1)}, bf16[1024,1152]{1,0:T(8,128)(2,1)S(1)}) fusion(f32[1024,1152]{1,0:T(8,128)} %fusion.78, f32[1024,1152]{1,0:T(8,128)} %fusion.79, bf16[1024,1024]{1,0:T(8,128)(2,1)} %bitcast.350, bf16[1152,1024]{1,0:T(8,128)(2,1)} %bitcast.398), kind=kOutput, calls=%fused_computation.3 | convolution fusion | flops 2433613824 | bytes 20971520 | tf_op jit(solution)/shard_map/dot_general | solution.py:79
  196.5 4.3 convolution_add_fusion
  204.4 4.9 fusion.84
  217.9 5.4 fusion.83
  230.8 4.7 fusion.80
  246.2 4.6 fusion.77
  254.1 4.5 convolution_add_fusion.4
  295.0 4.1 collective-permute-start.40
  302.5 36.0 %collective-permute-done.40 = bf16[2,144,1024]{2,1,0:T(8,128)(2,1)S(1)} collective-permute-done((bf16[2,144,1024]{2,1,0:T(8,128)(2,1)S(1)}, bf16[2,144,1024]{2,1,0:T(8,128)(2,1)S(1)}, u32[]{:S(2)}, u32[]{:S(2)}) %collective-permute-start.40) | collective-permute-done | bytes 589856 | tf_op jit(solution)/shard_map/ppermute | solution.py:18
  338.8 25.0 %collective-permute-done.34 = bf16[2,128,1152]{1,2,0:T(8,128)(2,1)S(1)} collective-permute-done((bf16[2,128,1152]{1,2,0:T(8,128)(2,1)S(1)}, bf16[2,128,1152]{1,2,0:T(8,128)(2,1)S(1)}, u32[]{:S(2)}, u32[]{:S(2)}) %collective-permute-start.34) | collective-permute-done | bytes 589856 | tf_op jit(solution)/shard_map/ppermute | solution.py:18
  364.0 11.6 %collective-permute-done.28 = bf16[2,128,1152]{1,2,0:T(8,128)(2,1)S(1)} collective-permute-done((bf16[2,128,1152]{1,2,0:T(8,128)(2,1)S(1)}, bf16[2,128,1152]{1,2,0:T(8,128)(2,1)S(1)}, u32[]{:S(2)}, u32[]{:S(2)}) %collective-permute-start.28) | collective-permute-done | bytes 589856 | tf_op jit(solution)/shard_map/ppermute | solution.py:18
  375.8 12.3 %collective-permute-done.35 = bf16[128,1152]{0,1:T(8,128)(2,1)S(1)} collective-permute-done((bf16[128,1152]{0,1:T(8,128)(2,1)S(1)}, bf16[128,1152]{0,1:T(8,128)(2,1)S(1)}, u32[]{:S(2)}, u32[]{:S(2)}) %collective-permute-start.35) | collective-permute-done | bytes 294944 | tf_op jit(solution)/shard_map/ppermute | solution.py:18
  390.8 6.2 %collective-permute-done.29 = bf16[128,1152]{0,1:T(8,128)(2,1)S(1)} collective-permute-done((bf16[128,1152]{0,1:T(8,128)(2,1)S(1)}, bf16[128,1152]{0,1:T(8,128)(2,1)S(1)}, u32[]{:S(2)}, u32[]{:S(2)}) %collective-permute-start.29) | collective-permute-done | bytes 294944 | tf_op jit(solution)/shard_map/ppermute | solution.py:18
  401.5 13.7 %collective-permute-done.2 = bf16[512,1024]{1,0:T(8,128)(2,1)} collective-permute-done((bf16[512,1024]{1,0:T(8,128)(2,1)S(1)}, bf16[512,1024]{1,0:T(8,128)(2,1)}, u32[]{:S(2)}, u32[]{:S(2)}) %collective-permute-start.2) | collective-permute-done | bytes 1048608 | tf_op jit(solution)/shard_map/ppermute | solution.py:18
  415.3 5.5 bitcast_add_fusion.5
  420.8 3.8 multiply_reduce_fusion
  428.4 5.2 fusion.21
  435.3 4.0 fusion.39
  443.7 5.3 fusion.4
  464.0 4.3 collective-permute-done.31
  470.2 13.1 %collective-permute-done.20 = bf16[8,32,1024]{2,1,0:T(8,128)(2,1)S(1)} collective-permute-done((bf16[8,32,1024]{2,1,0:T(8,128)(2,1)S(1)}, bf16[8,32,1024]{2,1,0:T(8,128)(2,1)S(1)}, u32[]{:S(2)}, u32[]{:S(2)}) %collective-permute-start.20) | collective-permute-done | bytes 524320 | tf_op jit(solution)/shard_map/ppermute | solution.py:18
  486.4 5.2 collective-permute-done.21
  494.5 5.0 collective-permute-done.22
  499.6 21.5 %collective-permute-done.12 = bf16[8,32,3072]{2,1,0:T(8,128)(2,1)S(1)} collective-permute-done((bf16[8,32,3072]{2,1,0:T(8,128)(2,1)S(1)}, bf16[8,32,3072]{2,1,0:T(8,128)(2,1)S(1)}, u32[]{:S(2)}, u32[]{:S(2)}) %collective-permute-start.12) | collective-permute-done | bytes 1572896 | tf_op jit(solution)/shard_map/ppermute | solution.py:18
  543.4 16.7 %collective-permute-done.14 = bf16[2,32,3072]{2,1,0:T(8,128)(2,1)S(1)} collective-permute-done((bf16[2,32,3072]{2,1,0:T(8,128)(2,1)S(1)}, bf16[2,32,3072]{2,1,0:T(8,128)(2,1)S(1)}, u32[]{:S(2)}, u32[]{:S(2)}) %collective-permute-start.14) | collective-permute-done | bytes 393248 | tf_op jit(solution)/shard_map/ppermute | solution.py:18
  560.3 6.8 %collective-permute-done.15 = bf16[32,3072]{1,0:T(8,128)(2,1)S(1)} collective-permute-done((bf16[32,3072]{1,0:T(8,128)(2,1)S(1)}, bf16[32,3072]{1,0:T(8,128)(2,1)S(1)}, u32[]{:S(2)}, u32[]{:S(2)}) %collective-permute-start.15) | collective-permute-done | bytes 196640 | tf_op jit(solution)/shard_map/ppermute | solution.py:18
  569.4 5.3 collective-permute-done.17
  (359 shorter events, 167.9 us)
Async XLA Ops:
  203.8 86.7 %collective-permute-start.39 = (bf16[2,2,144,1024]{3,2,1,0:T(8,128)(2,1)}, bf16[2,2,144,1024]{3,2,1,0:T(8,128)(2,1)}, u32[]{:S(2)}, u32[]{:S(2)}) collective-permute-start(bf16[2,2,144,1024]{3,2,1,0:T(8,128)(2,1)} %fusion.34), channel_id=1, source_target_pairs={{0,1},{1,0},{2,3},{3,2},{4,5},{5,4},{6,7},{7,6},{8,9},{9,8},{10,11... | collective-permute-start | bytes 3538952 | tf_op jit(solution)/shard_map/ppermute | solution.py:18
  216.4 78.6 %collective-permute-start.33 = (bf16[2,2,128,1152]{2,3,1,0:T(8,128)(2,1)}, bf16[2,2,128,1152]{2,3,1,0:T(8,128)(2,1)}, u32[]{:S(2)}, u32[]{:S(2)}) collective-permute-start(bf16[2,2,128,1152]{2,3,1,0:T(8,128)(2,1)} %bitcast.357), channel_id=1, source_target_pairs={{0,1},{1,0},{2,3},{3,2},{4,5},{5,4},{6,7},{7,6},{8,9},{9,8},{10,11... | collective-permute-start | bytes 3538952 | tf_op jit(solution)/shard_map/ppermute | solution.py:18
  230.2 70.4 %collective-permute-start.27 = (bf16[2,2,128,1152]{2,3,1,0:T(8,128)(2,1)}, bf16[2,2,128,1152]{2,3,1,0:T(8,128)(2,1)}, u32[]{:S(2)}, u32[]{:S(2)}) collective-permute-start(bf16[2,2,128,1152]{2,3,1,0:T(8,128)(2,1)} %bitcast.262), channel_id=1, source_target_pairs={{0,1},{1,0},{2,3},{3,2},{4,5},{5,4},{6,7},{7,6},{8,9},{9,8},{10,11... | collective-permute-start | bytes 3538952 | tf_op jit(solution)/shard_map/ppermute | solution.py:18
  238.5 47.3 %collective-permute-start.1 = (bf16[512,1024]{1,0:T(8,128)(2,1)}, bf16[512,1024]{1,0:T(8,128)(2,1)}, u32[]{:S(2)}, u32[]{:S(2)}) collective-permute-start(bf16[512,1024]{1,0:T(8,128)(2,1)} %slice.180), channel_id=1, source_target_pairs={{0,8},{8,0},{16,24},{24,16},{1,9},{9,1},{17,25},{25,17},{2,10},{10... | collective-permute-start | bytes 3145736 | tf_op jit(solution)/shard_map/ppermute | solution.py:18
  245.8 42.5 %collective-permute-start.4 = (bf16[512,1024]{1,0:T(8,128)(2,1)}, bf16[512,1024]{1,0:T(8,128)(2,1)}, u32[]{:S(2)}, u32[]{:S(2)}) collective-permute-start(bf16[512,1024]{1,0:T(8,128)(2,1)} %slice.178), channel_id=1, source_target_pairs={{0,8},{8,0},{16,24},{24,16},{1,9},{9,1},{17,25},{25,17},{2,10},{10... | collective-permute-start | bytes 3145736 | tf_op jit(solution)/shard_map/ppermute | solution.py:18
  285.8 114.3 %collective-permute-start = (bf16[512,1024]{1,0:T(8,128)(2,1)}, bf16[512,1024]{1,0:T(8,128)(2,1)S(1)}, u32[]{:S(2)}, u32[]{:S(2)}) collective-permute-start(bf16[512,1024]{1,0:T(8,128)(2,1)} %slice.181), channel_id=1, source_target_pairs={{0,8},{8,0},{16,24},{24,16},{1,9},{9,1},{17,25},{25,17},{2,10},{10... | collective-permute-start | bytes 3145736 | tf_op jit(solution)/shard_map/ppermute | solution.py:18
  288.2 109.9 %collective-permute-start.3 = (bf16[512,1024]{1,0:T(8,128)(2,1)}, bf16[512,1024]{1,0:T(8,128)(2,1)S(1)}, u32[]{:S(2)}, u32[]{:S(2)}) collective-permute-start(bf16[512,1024]{1,0:T(8,128)(2,1)} %slice.179), channel_id=1, source_target_pairs={{0,8},{8,0},{16,24},{24,16},{1,9},{9,1},{17,25},{25,17},{2,10},{10... | collective-permute-start | bytes 3145736 | tf_op jit(solution)/shard_map/ppermute | solution.py:18
  290.6 108.3 %collective-permute-start.5 = (bf16[512,1024]{1,0:T(8,128)(2,1)S(1)}, bf16[512,1024]{1,0:T(8,128)(2,1)S(1)}, u32[]{:S(2)}, u32[]{:S(2)}) collective-permute-start(bf16[512,1024]{1,0:T(8,128)(2,1)S(1)} %fusion.22), channel_id=1, source_target_pairs={{0,16},{8,24},{16,0},{24,8},{1,17},{9,25},{17,1},{25,9},{2,18},{10... | collective-permute-start | bytes 3145736 | tf_op jit(solution)/shard_map/ppermute | solution.py:18
  295.0 43.5 %collective-permute-start.40 = (bf16[2,144,1024]{2,1,0:T(8,128)(2,1)S(1)}, bf16[2,144,1024]{2,1,0:T(8,128)(2,1)S(1)}, u32[]{:S(2)}, u32[]{:S(2)}) collective-permute-start(bf16[2,144,1024]{2,1,0:T(8,128)(2,1)S(1)} %dynamic-slice_bitcast_fusion.1), channel_id=1, source_target_pairs={{0,4},{1,5},{2,6},{3,7},{4,0},{5,1},{6,2},{7,3},{8,12},{9,13},{10,... | collective-permute-start | bytes 1769480 | tf_op jit(solution)/shard_map/ppermute | solution.py:18
  300.7 63.1 %collective-permute-start.34 = (bf16[2,128,1152]{1,2,0:T(8,128)(2,1)S(1)}, bf16[2,128,1152]{1,2,0:T(8,128)(2,1)S(1)}, u32[]{:S(2)}, u32[]{:S(2)}) collective-permute-start(bf16[2,128,1152]{1,2,0:T(8,128)(2,1)S(1)} %dynamic-slice_bitcast_fusion.2), channel_id=1, source_target_pairs={{0,4},{1,5},{2,6},{3,7},{4,0},{5,1},{6,2},{7,3},{8,12},{9,13},{10,... | collective-permute-start | bytes 1769480 | tf_op jit(solution)/shard_map/ppermute | solution.py:18
  338.5 37.1 %collective-permute-start.28 = (bf16[2,128,1152]{1,2,0:T(8,128)(2,1)S(1)}, bf16[2,128,1152]{1,2,0:T(8,128)(2,1)S(1)}, u32[]{:S(2)}, u32[]{:S(2)}) collective-permute-start(bf16[2,128,1152]{1,2,0:T(8,128)(2,1)S(1)} %dynamic-slice_bitcast_fusion.3), channel_id=1, source_target_pairs={{0,4},{1,5},{2,6},{3,7},{4,0},{5,1},{6,2},{7,3},{8,12},{9,13},{10,... | collective-permute-start | bytes 1769480 | tf_op jit(solution)/shard_map/ppermute | solution.py:18
  363.8 25.4 %collective-permute-start.41 = (bf16[144,1024]{1,0:T(8,128)(2,1)S(1)}, bf16[144,1024]{1,0:T(8,128)(2,1)S(1)}, u32[]{:S(2)}, u32[]{:S(2)}) collective-permute-start(bf16[144,1024]{1,0:T(8,128)(2,1)S(1)} %dynamic-slice_bitcast_fusion.6), channel_id=1, source_target_pairs={{0,2},{1,3},{2,0},{3,1},{4,6},{5,7},{6,4},{7,5},{8,10},{9,11},{10,... | collective-permute-start | bytes 884744 | tf_op jit(solution)/shard_map/ppermute | solution.py:18
  375.6 12.5 %collective-permute-start.35 = (bf16[128,1152]{0,1:T(8,128)(2,1)S(1)}, bf16[128,1152]{0,1:T(8,128)(2,1)S(1)}, u32[]{:S(2)}, u32[]{:S(2)}) collective-permute-start(bf16[128,1152]{0,1:T(8,128)(2,1)S(1)} %dynamic-slice_bitcast_fusion.7), channel_id=1, source_target_pairs={{0,2},{1,3},{2,0},{3,1},{4,6},{5,7},{6,4},{7,5},{8,10},{9,11},{10,... | collective-permute-start | bytes 884744 | tf_op jit(solution)/shard_map/ppermute | solution.py:18
  388.1 8.9 %collective-permute-start.29 = (bf16[128,1152]{0,1:T(8,128)(2,1)S(1)}, bf16[128,1152]{0,1:T(8,128)(2,1)S(1)}, u32[]{:S(2)}, u32[]{:S(2)}) collective-permute-start(bf16[128,1152]{0,1:T(8,128)(2,1)S(1)} %dynamic-slice_bitcast_fusion.8), channel_id=1, source_target_pairs={{0,2},{1,3},{2,0},{3,1},{4,6},{5,7},{6,4},{7,5},{8,10},{9,11},{10,... | collective-permute-start | bytes 884744 | tf_op jit(solution)/shard_map/ppermute | solution.py:18
  389.2 26.1 %collective-permute-start.2 = (bf16[512,1024]{1,0:T(8,128)(2,1)S(1)}, bf16[512,1024]{1,0:T(8,128)(2,1)}, u32[]{:S(2)}, u32[]{:S(2)}) collective-permute-start(bf16[512,1024]{1,0:T(8,128)(2,1)S(1)} %fusion.24), channel_id=1, source_target_pairs={{0,16},{8,24},{16,0},{24,8},{1,17},{9,25},{17,1},{25,9},{2,18},{10... | collective-permute-start | bytes 3145736 | tf_op jit(solution)/shard_map/ppermute | solution.py:18
  397.1 65.0 %collective-permute-start.42 = (bf16[144,1024]{1,0:T(8,128)(2,1)}, bf16[144,1024]{1,0:T(8,128)(2,1)}, u32[]{:S(2)}, u32[]{:S(2)}) collective-permute-start(bf16[144,1024]{1,0:T(8,128)(2,1)} %get-tuple-element.43), channel_id=1, source_target_pairs={{0,8},{8,0},{16,24},{24,16},{1,9},{9,1},{17,25},{25,17},{2,10},{10... | collective-permute-start | bytes 884744 | tf_op jit(solution)/shard_map/ppermute | solution.py:18
  398.1 65.3 %collective-permute-start.43 = (bf16[144,1024]{1,0:T(8,128)(2,1)}, bf16[144,1024]{1,0:T(8,128)(2,1)S(1)}, u32[]{:S(2)}, u32[]{:S(2)}) collective-permute-start(bf16[144,1024]{1,0:T(8,128)(2,1)} %get-tuple-element.43), channel_id=1, source_target_pairs={{0,16},{8,24},{16,0},{24,8},{1,17},{9,25},{17,1},{25,9},{2,18},{10... | collective-permute-start | bytes 884744 | tf_op jit(solution)/shard_map/ppermute | solution.py:18
  398.9 60.0 %collective-permute-start.36 = (bf16[128,1152]{0,1:T(8,128)(2,1)}, bf16[128,1152]{0,1:T(8,128)(2,1)}, u32[]{:S(2)}, u32[]{:S(2)}) collective-permute-start(bf16[128,1152]{0,1:T(8,128)(2,1)} %get-tuple-element.45), channel_id=1, source_target_pairs={{0,8},{8,0},{16,24},{24,16},{1,9},{9,1},{17,25},{25,17},{2,10},{10... | collective-permute-start | bytes 884744 | tf_op jit(solution)/shard_map/ppermute | solution.py:18
  400.1 60.6 %collective-permute-start.37 = (bf16[128,1152]{0,1:T(8,128)(2,1)}, bf16[128,1152]{0,1:T(8,128)(2,1)}, u32[]{:S(2)}, u32[]{:S(2)}) collective-permute-start(bf16[128,1152]{0,1:T(8,128)(2,1)} %get-tuple-element.45), channel_id=1, source_target_pairs={{0,16},{8,24},{16,0},{24,8},{1,17},{9,25},{17,1},{25,9},{2,18},{10... | collective-permute-start | bytes 884744 | tf_op jit(solution)/shard_map/ppermute | solution.py:18
  433.7 8.0 %collective-permute-start.6 = (f32[2,2,8,128]{3,2,1,0:T(8,128)S(1)}, f32[2,2,8,128]{3,2,1,0:T(8,128)S(1)}, u32[]{:S(2)}, u32[]{:S(2)}) collective-permute-start(f32[2,2,8,128]{3,2,1,0:T(8,128)S(1)} %fusion.56), channel_id=1, source_target_pairs={{0,1},{1,0},{2,3},{3,2},{4,5},{5,4},{6,7},{7,6},{8,9},{9,8},{10,11... | collective-permute-start | bytes 49160 | tf_op jit(solution)/shard_map/ppermute | solution.py:18
  458.9 9.4 %collective-permute-start.31 = (bf16[128,1152]{0,1:T(8,128)(2,1)S(1)}, bf16[128,1152]{0,1:T(8,128)(2,1)S(1)}, u32[]{:S(2)}, u32[]{:S(2)}) collective-permute-start(bf16[128,1152]{0,1:T(8,128)(2,1)S(1)} %copy-done.39), channel_id=1, source_target_pairs={{0,16},{8,24},{16,0},{24,8},{1,17},{9,25},{17,1},{25,9},{2,18},{10... | collective-permute-start | bytes 884744 | tf_op jit(solution)/shard_map/ppermute | solution.py:18
  460.8 23.4 %collective-permute-start.11 = (bf16[8,2,32,3072]{3,2,1,0:T(8,128)(2,1)S(1)}, bf16[8,2,32,3072]{3,2,1,0:T(8,128)(2,1)S(1)}, u32[]{:S(2)}, u32[]{:S(2)}) collective-permute-start(bf16[8,2,32,3072]{3,2,1,0:T(8,128)(2,1)S(1)} %fusion.3), channel_id=1, source_target_pairs={{0,8},{8,0},{16,24},{24,16},{1,9},{9,1},{17,25},{25,17},{2,10},{10... | collective-permute-start | bytes 9437192 | tf_op jit(solution)/shard_map/ppermute | solution.py:18
  463.7 22.6 %collective-permute-start.44 = (bf16[144,1024]{1,0:T(8,128)(2,1)S(1)}, bf16[144,1024]{1,0:T(8,128)(2,1)S(1)}, u32[]{:S(2)}, u32[]{:S(2)}) collective-permute-start(bf16[144,1024]{1,0:T(8,128)(2,1)S(1)} %collective-permute-done.43), channel_id=1, source_target_pairs={{0,8},{8,0},{16,24},{24,16},{1,9},{9,1},{17,25},{25,17},{2,10},{10... | collective-permute-start | bytes 884744 | tf_op jit(solution)/shard_map/ppermute | solution.py:18
  468.3 18.0 %collective-permute-start.32 = (bf16[128,1152]{0,1:T(8,128)(2,1)S(1)}, bf16[128,1152]{0,1:T(8,128)(2,1)S(1)}, u32[]{:S(2)}, u32[]{:S(2)}) collective-permute-start(bf16[128,1152]{0,1:T(8,128)(2,1)S(1)} %collective-permute-done.31), channel_id=1, source_target_pairs={{0,8},{8,0},{16,24},{24,16},{1,9},{9,1},{17,25},{25,17},{2,10},{10... | collective-permute-start | bytes 884744 | tf_op jit(solution)/shard_map/ppermute | solution.py:18
  468.9 14.4 %collective-permute-start.20 = (bf16[8,32,1024]{2,1,0:T(8,128)(2,1)S(1)}, bf16[8,32,1024]{2,1,0:T(8,128)(2,1)S(1)}, u32[]{:S(2)}, u32[]{:S(2)}) collective-permute-start(bf16[8,32,1024]{2,1,0:T(8,128)(2,1)S(1)} %dynamic-slice_bitcast_fusion.4), channel_id=1, source_target_pairs={{0,16},{8,24},{16,0},{24,8},{1,17},{9,25},{17,1},{25,9},{2,18},{10... | collective-permute-start | bytes 1572872 | tf_op jit(solution)/shard_map/ppermute | solution.py:18
  483.5 8.0 %collective-permute-start.21 = (bf16[2,2,32,1024]{3,2,1,0:T(8,128)(2,1)S(1)}, bf16[2,2,32,1024]{3,2,1,0:T(8,128)(2,1)S(1)}, u32[]{:S(2)}, u32[]{:S(2)}) collective-permute-start(bf16[2,2,32,1024]{3,2,1,0:T(8,128)(2,1)S(1)} %fusion.51), channel_id=1, source_target_pairs={{0,1},{1,0},{2,3},{3,2},{4,5},{5,4},{6,7},{7,6},{8,9},{9,8},{10,11... | collective-permute-start | bytes 786440 | tf_op jit(solution)/shard_map/ppermute | solution.py:18
  485.3 35.8 %collective-permute-start.12 = (bf16[8,32,3072]{2,1,0:T(8,128)(2,1)S(1)}, bf16[8,32,3072]{2,1,0:T(8,128)(2,1)S(1)}, u32[]{:S(2)}, u32[]{:S(2)}) collective-permute-start(bf16[8,32,3072]{2,1,0:T(8,128)(2,1)S(1)} %dynamic-slice_bitcast_fusion), channel_id=1, source_target_pairs={{0,16},{8,24},{16,0},{24,8},{1,17},{9,25},{17,1},{25,9},{2,18},{10... | collective-permute-start | bytes 4718600 | tf_op jit(solution)/shard_map/ppermute | solution.py:18
  499.6 24.8 %collective-permute-start.23 = (bf16[32,1024]{1,0:T(8,128)(2,1)S(1)}, bf16[32,1024]{1,0:T(8,128)(2,1)S(1)}, u32[]{:S(2)}, u32[]{:S(2)}) collective-permute-start(bf16[32,1024]{1,0:T(8,128)(2,1)S(1)} %dynamic-slice_bitcast_fusion.11), channel_id=1, source_target_pairs={{0,2},{1,3},{2,0},{3,1},{4,6},{5,7},{6,4},{7,5},{8,10},{9,11},{10,... | collective-permute-start | bytes 196616 | tf_op jit(solution)/shard_map/ppermute | solution.py:18
  522.7 18.3 %collective-permute-start.13 = (bf16[2,2,32,3072]{3,2,1,0:T(8,128)(2,1)}, bf16[2,2,32,3072]{3,2,1,0:T(8,128)(2,1)}, u32[]{:S(2)}, u32[]{:S(2)}) collective-permute-start(bf16[2,2,32,3072]{3,2,1,0:T(8,128)(2,1)} %fusion.40), channel_id=1, source_target_pairs={{0,1},{1,0},{2,3},{3,2},{4,5},{5,4},{6,7},{7,6},{8,9},{9,8},{10,11... | collective-permute-start | bytes 2359304 | tf_op jit(solution)/shard_map/ppermute | solution.py:18
  524.4 13.2 %collective-permute-start.25 = (bf16[32,1024]{1,0:T(8,128)(2,1)S(1)}, bf16[32,1024]{1,0:T(8,128)(2,1)S(1)}, u32[]{:S(2)}, u32[]{:S(2)}) collective-permute-start(bf16[32,1024]{1,0:T(8,128)(2,1)S(1)} %get-tuple-element.49), channel_id=1, source_target_pairs={{0,16},{8,24},{16,0},{24,8},{1,17},{9,25},{17,1},{25,9},{2,18},{10... | collective-permute-start | bytes 196616 | tf_op jit(solution)/shard_map/ppermute | solution.py:18
  537.6 22.7 %collective-permute-start.26 = (bf16[32,1024]{1,0:T(8,128)(2,1)S(1)}, bf16[32,1024]{1,0:T(8,128)(2,1)S(1)}, u32[]{:S(2)}, u32[]{:S(2)}) collective-permute-start(bf16[32,1024]{1,0:T(8,128)(2,1)S(1)} %collective-permute-done.25), channel_id=1, source_target_pairs={{0,8},{8,0},{16,24},{24,16},{1,9},{9,1},{17,25},{25,17},{2,10},{10... | collective-permute-start | bytes 196616 | tf_op jit(solution)/shard_map/ppermute | solution.py:18
  542.3 17.8 %collective-permute-start.14 = (bf16[2,32,3072]{2,1,0:T(8,128)(2,1)S(1)}, bf16[2,32,3072]{2,1,0:T(8,128)(2,1)S(1)}, u32[]{:S(2)}, u32[]{:S(2)}) collective-permute-start(bf16[2,32,3072]{2,1,0:T(8,128)(2,1)S(1)} %dynamic-slice_bitcast_fusion.5), channel_id=1, source_target_pairs={{0,4},{1,5},{2,6},{3,7},{4,0},{5,1},{6,2},{7,3},{8,12},{9,13},{10,... | collective-permute-start | bytes 1179656 | tf_op jit(solution)/shard_map/ppermute | solution.py:18
  (85 other events, 478.0 us)

commit v3 on v2

--- a/solution.py
+++ b/solution.py
@@ -13,60 +13,6 @@
 MESH = pl.DeviceIdType.MESH
 
 
-def hop(values, axis, bit):
-    size = lax.axis_size(axis)
-    return lax.ppermute(values, axis, [(at, at ^ bit) for at in range(size)])
-
-
-def after(values, *earlier):
-    return lax.optimization_barrier((values, *earlier))[0]
-
-
-def gather_bits():
-    size = lax.axis_size("fsdp")
-    bits = [1 << k for k in range(size.bit_length() - 1)]
-    return bits[1:] + bits[:1]
-
-
-def gather_pieces(own):
-    pieces = {0: own}
-    for bit in gather_bits():
-        for offset in list(pieces):
-            pieces[offset ^ bit] = hop(pieces[offset], "fsdp", bit)
-    return pieces
-
-
-def put(target, block, index):
-    return lax.dynamic_update_slice(target, block, index + (0,) * (target.ndim - len(index)))
-
-
-def in_order(pieces, place):
-    shards = len(pieces)
-    whole = jnp.zeros((shards, *pieces[0].shape), pieces[0].dtype)
-    for offset, piece in pieces.items():
-        whole = put(whole, piece[None], (place ^ offset,))
-    return whole
-
-
-def reduce_pieces(whole, kind=LOW):
-    place = lax.axis_index("fsdp")
-    shards = whole.shape[0]
-    bits = gather_bits()[::-1]
-    top = shards.bit_length() - 1
-    rest = whole.shape[1:]
-    held = whole.reshape((2,) * top + rest)
-    axes = [1 << k for k in reversed(range(top))]
-    for bit in bits:
-        axis = axes.index(bit)
-        mine = jnp.where((place & bit) != 0, 1, 0)
-        sent = lax.dynamic_index_in_dim(held, 1 - mine, axis, keepdims=False).astype(kind)
-        kept = lax.dynamic_index_in_dim(held, mine, axis, keepdims=False).astype(F32)
-        total = kept + hop(sent, "fsdp", bit).astype(F32)
-        axes.pop(axis)
-        held = total.astype(kind) if axes else total
-    return held
-
-
 def rms_scale(values):
     return lax.rsqrt(jnp.mean(values * values, axis=-1, keepdims=True) + EPSILON)
 
@@ -88,72 +34,6 @@
     return scale * (
         scaled - values * scale * scale * jnp.mean(scaled * values, axis=-1, keepdims=True)
     )
-
-
-def sum_over_rep(own_and_core, across):
-    rows = own_and_core.shape[0] // 2
-    near = hop(own_and_core[rows:].astype(LOW), "rep", 1).astype(F32)
-    far = hop(across[rows:].astype(LOW), "rep", 1).astype(F32)
-    own = own_and_core[:rows] + near
-    other = (across[:rows] + far).astype(LOW)
-    return own + hop(other, "rep", 2).astype(F32)
-
-
-def spread_over_rep(values):
-    near = hop(values, "rep", 1)
-    across = hop(values, "rep", 2)
-    return jnp.concatenate([values, near]), jnp.concatenate([across, hop(across, "rep", 1)])
-
-
-def share_quarters(quarter):
-    rep = lax.axis_index("rep")
-    near = hop(quarter, "rep", 1)
-    across = hop(quarter, "rep", 2)
-    corner = hop(across, "rep", 1)
-    whole = jnp.zeros((4, *quarter.shape), quarter.dtype)
-    for offset, block in enumerate((quarter, near, across, corner)):
-        whole = put(whole, block[None], (rep ^ offset,))
-    return whole
-
-
-def gather_full(weight, *earlier):
-    rep = lax.axis_index("rep")
-    place = lax.axis_index("fsdp")
-    rows, cols = weight.shape
-    quarter = rows // 4
-    own = lax.dynamic_slice_in_dim(weight, rep * quarter, quarter, 0)
-    pieces = gather_pieces(after(own, *earlier) if earlier else own)
-    shards = len(pieces)
-    whole = jnp.zeros((shards, 4, quarter, cols), weight.dtype)
-    whole = put(whole, weight.reshape(1, 4, quarter, cols), (place,))
-    for flip in (0, 1):
-        group = {o: p for o, p in pieces.items() if o & 1 == flip and o}
-        offsets = sorted(group)
-        stacked = jnp.stack([group[o] for o in offsets])
-        across = hop(stacked, "rep", 2)
-        near = hop(stacked, "rep", 1)
-        corner = hop(across, "rep", 1)
-        for turn, block in enumerate((stacked, near, across, corner)):
-            for at, offset in enumerate(offsets):
-                whole = put(whole, block[at][None, None], (place ^ offset, rep ^ turn))
-    return whole.reshape(shards * rows, cols), pieces
-
-
-def reduce_full(grad):
-    rep = lax.axis_index("rep")
-    shards = lax.axis_size("fsdp")
-    rows, cols = grad.shape
-    quarter = rows // shards // 4
-    held = grad.reshape(shards, 2, 2, quarter, cols)
-    core, side = rep & 1, (rep >> 1) & 1
-    sent = lax.dynamic_index_in_dim(held, 1 - core, 2, keepdims=False).astype(LOW)
-    kept = lax.dynamic_index_in_dim(held, core, 2, keepdims=False)
-    pair = (kept.astype(F32) + hop(sent, "rep", 1).astype(F32)).astype(LOW)
-    sent = lax.dynamic_index_in_dim(pair, 1 - side, 1, keepdims=False)
-    kept = lax.dynamic_index_in_dim(pair, side, 1, keepdims=False)
-    four = kept.astype(F32) + hop(sent, "rep", 2).astype(F32)
-    own = reduce_pieces(four).astype(LOW)
-    return share_quarters(own).reshape(4 * quarter, cols).astype(F32)
 
 
 def flipped(index, offset):
@@ -473,6 +353,438 @@
     )(rows, cot, small, w_in, w_out, gate, up, down)
 
 
+def add_into(target, *others):
+    rows = target.shape[-2]
+    step = 16 if rows % 16 == 0 else rows
+    lead = target.shape[:-2]
+
+    @pl.loop(0, rows // step)
+    def _(at):
+        held = pl.ds(pl.multiple_of(at * step, step), step)
+        index = (slice(None),) * len(lead) + (held,)
+        total = target[index].astype(F32)
+        for other in others:
+            total = total + other[index].astype(F32)
+        target[index] = total.astype(target.dtype)
+
+
+class Collect:
+    def __init__(self, copies, shards, sent_at, own_at, near_in, far_in):
+        self.copies = copies
+        self.sent_at, self.own_at = sent_at, own_at
+        self.near_in, self.far_in = near_in, far_in
+        self.order = [*range(2, shards, 2), 0]
+        self.arriving = {}
+        self.far = {}
+
+    def near(self, offset):
+        copies = self.copies
+        self.arriving[offset] = copies.send(
+            self.sent_at(offset + 1), self.near_in.at[offset // 2], 0, 1
+        )
+
+    def near_all(self):
+        for offset in self.order:
+            self.near(offset)
+
+    def combine(self, offset):
+        self.arriving[offset].wait_recv()
+        own = self.own_at(offset)
+        add_into(own, self.near_in.at[offset // 2])
+        if offset:
+            self.far[offset] = self.copies.send(
+                own, self.far_in.at[offset // 2 - 1], 0, offset
+            )
+
+    def combine_all(self):
+        for offset in self.order:
+            self.combine(offset)
+
+    def total(self):
+        for copy in self.far.values():
+            copy.wait_recv()
+        own = self.own_at(0)
+        add_into(own, *[self.far_in.at[k] for k in range(len(self.far))])
+        return own
+
+
+class Share:
+    def __init__(self, copies, local, source, target_at):
+        self.copies = copies
+        self.target_at = target_at
+        here = target_at(copies.rep)
+        self.across = copies.send(source, here, 2, 0)
+        self.core = [copies.send(source, here, 1, 0)]
+        self.own = local.copy(source, here)
+
+    def forward(self):
+        self.across.wait_recv()
+        block = self.target_at(flipped(self.copies.rep, 2))
+        self.core.append(self.copies.send(block, block, 1, 0))
+
+    def finish(self):
+        for copy in self.core:
+            copy.wait_recv()
+        self.own.wait()
+
+
+class CollectAll:
+    def __init__(self, copies, shards, width, parts, core_in, cross_in, near_in, far_in):
+        self.copies = copies
+        self.width = width
+        self.parts, self.core_in, self.cross_in = parts, core_in, cross_in
+        place = copies.place
+        self.collect = Collect(
+            copies,
+            shards,
+            lambda offset: parts.at[0, flipped(place, offset)],
+            lambda offset: parts.at[0, flipped(place, offset)],
+            near_in,
+            far_in,
+        )
+        self.core = {}
+        self.cross = {}
+        self.order = [o + 1 for o in self.collect.order] + self.collect.order
+
+    def compute(self, turn, left, right):
+        rep = flipped(self.copies.rep, turn)
+        shards, rows, _ = self.parts.shape[1:]
+        for at in range(0, self.width, 256):
+            columns = pl.ds(pl.multiple_of(rep * self.width + at, 256), 256)
+            block = dot_first(left[...], right[:, columns]).astype(LOW)
+            self.parts[turn, :, :, at : at + 256] = block.reshape(shards, rows, 256)
+
+    def to_core(self, turn):
+        self.core[turn - 1] = self.copies.send(
+            self.parts.at[turn], self.core_in.at[turn // 2], 1, 0
+        )
+
+    def to_cross(self):
+        self.core[2].wait_recv()
+        place = self.copies.place
+        for offset in self.order:
+            block = self.parts.at[2, flipped(place, offset)]
+            add_into(block, self.core_in.at[1, flipped(place, offset)])
+            self.cross[offset] = self.copies.send(
+                block, self.cross_in.at[flipped(place, offset)], 2, 0
+            )
+        self.core[0].wait_recv()
+
+    def arrive(self, offset):
+        self.cross[offset].wait_recv()
+        shard = flipped(self.copies.place, offset)
+        add_into(self.parts.at[0, shard], self.core_in.at[0, shard], self.cross_in.at[shard])
+
+    def near_all(self):
+        for offset in self.collect.order:
+            self.arrive(offset + 1)
+            self.collect.near(offset)
+
+    def combine_all(self):
+        for offset in self.collect.order:
+            self.arrive(offset)
+            self.collect.combine(offset)
+
+
+def backward_kernel(
+    slot,
+    rows_ref, cot_ref, gains_ref, in_ref, out_ref, d_act_ref, ffn_ref, down_ref, gate_ref, up_ref,
+    outputs_ref, d_rows_ref, down_sum, gate_sum, up_sum, in_sum, out_sum, small_sum, ffn_in,
+    v_in, v_out, act_one, part_b, part_c, part_x, mixer_in, hstate, d_act, d_core, d_cross,
+    ffn_part, d_hstate, d_mixer, d_proj,
+    down_own, down_near, down_far, gate_own, gate_near, gate_far, up_own, up_near, up_far,
+    w_out_parts, w_out_core, w_out_cross, w_out_near, w_out_far,
+    w_in_parts, w_in_core, w_in_cross, w_in_near, w_in_far,
+    small, small_in, send_sems, recv_sems, local_sems,
+):
+    rows, features = rows_ref.shape
+    shards = gate_ref.shape[0]
+    copies = Copies(send_sems, recv_sems)
+    local = Local(local_sems)
+    place, rep = copies.place, copies.rep
+    far = list(range(2, shards, 2))
+    bits = [1 << k for k in range(1, shards.bit_length() - 1)]
+    copies.meet([(0, offset) for offset in [*far, 1]] + [(1, 0), (2, 0)])
+
+    d_near = [copies.send(d_act_ref.at[turn], d_core.at[turn // 2], 1, 0) for turn in (3, 1)]
+    d_own = [local.copy(d_act_ref.at[turn], d_act.at[turn // 2]) for turn in (2, 0)]
+    load_in = local.copy(in_ref, v_in)
+    load_out = local.copy(out_ref, v_out)
+
+    def collector(source, own, near, far_in):
+        loads = [
+            local.copy(source.at[flipped(place, offset)], own.at[offset // 2])
+            for offset in range(0, shards, 2)
+        ]
+        return loads, Collect(
+            copies,
+            shards,
+            lambda offset: source.at[flipped(place, offset)],
+            lambda offset: own.at[offset // 2],
+            near,
+            far_in,
+        )
+
+    down_loads, down = collector(down_ref, down_own, down_near, down_far)
+    gate_loads, gate = collector(gate_ref, gate_own, gate_near, gate_far)
+    up_loads, up = collector(up_ref, up_own, up_near, up_far)
+    down.near_all()
+    gate.near_all()
+
+    gain_one, gain_two = gains_ref[0:1], gains_ref[1:2]
+
+    def first(at):
+        act_one[at] = normed(rows_ref[at].astype(F32), gain_one).astype(LOW)
+
+    d_own[0].wait()
+    d_near[0].wait_recv()
+    d_far = []
+    for start in range(0, rows, slot):
+        held = slice(start, start + slot)
+        add_into(d_act.at[1, held], d_core.at[1, held])
+        d_far.append(copies.send(d_act.at[1, held], d_cross.at[held], 2, 0))
+    ffn_near = [copies.send(ffn_ref.at[turn], ffn_in.at[turn // 2], 1, 0) for turn in (3, 1)]
+    ffn_own = local.copy(ffn_ref.at[2], ffn_part)
+    row_loop(rows, 64, first)
+
+    load_in.wait()
+    width = features // 4
+    for part in range(4):
+        at = part * width
+        lanes = slice(at, at + width)
+        b_now, c_now, x_now, _, convolved = mixer_columns(
+            act_one[...], v_in, gains_ref, at, width, features, slot
+        )
+        part_b[:, lanes] = b_now
+        part_c[:, lanes] = c_now
+        part_x[:, lanes] = x_now
+        mixer_in[:, lanes] = (c_now * convolved).astype(LOW)
+        if part == 1:
+            for copy in down_loads:
+                copy.wait()
+            down.combine_all()
+            up.near_all()
+    load_out.wait()
+    for start in range(0, rows, slot):
+        held = slice(start, start + slot)
+        hstate[held] = rows_ref[held].astype(F32) + dot(
+            mixer_in[held], v_out[...].reshape(features, features)
+        )
+
+    ffn_own.wait()
+    ffn_near[0].wait_recv()
+    load = local.copy(ffn_in.at[1], d_mixer)
+    load.wait()
+    add_into(ffn_part, d_mixer)
+    load_cot = local.copy(cot_ref, d_mixer)
+    ffn_across = copies.send(ffn_part, ffn_in.at[2], 2, 0)
+    for copy in gate_loads:
+        copy.wait()
+    gate.combine_all()
+
+    d_own[1].wait()
+    d_near[1].wait_recv()
+    small[0] = jnp.zeros((8, features), F32)
+
+    def second(at):
+        d_now = (
+            d_act[0, at].astype(F32) + d_core[0, at].astype(F32) + d_cross[at].astype(F32)
+        )
+        values = hstate[at]
+        scale = rms_scale(values)
+        small[0, 1:2] += jnp.sum(d_now * values * scale, axis=0, keepdims=True)
+        d_values = d_mixer[at].astype(F32) + norm_back(d_now, values, scale, gain_two)
+        d_hstate[at] = d_values
+        d_mixer[at] = d_values.astype(LOW)
+
+    for copy in d_far:
+        copy.wait_recv()
+    load_cot.wait()
+    row_loop(rows, 64, second)
+
+    w_out = CollectAll(
+        copies, shards, features // 4, w_out_parts, w_out_core, w_out_cross, w_out_near, w_out_far
+    )
+    w_in = CollectAll(
+        copies, shards, 3 * features // 4, w_in_parts, w_in_core, w_in_cross, w_in_near, w_in_far
+    )
+    for turn in (3, 1):
+        w_out.compute(turn, mixer_in, d_mixer)
+        w_out.to_core(turn)
+    for turn in (2, 0):
+        w_out.compute(turn, mixer_in, d_mixer)
+
+    per = shards * width // features
+    for part in range(4):
+        at = part * width
+        lanes = slice(at, at + width)
+        block = v_out[part * per : (part + 1) * per].reshape(width, features)
+        d_mixin = dot_last(d_mixer[...], block)
+        taps = [gains_ref[2 + k : 3 + k, lanes] for k in range(3)]
+        for start in range(0, rows, slot):
+            held = slice(start, start + slot)
+            d_mix = d_mixin[held]
+            b_now, c_now, x_now = part_b[held, lanes], part_c[held, lanes], part_x[held, lanes]
+            product = b_now * x_now
+            before = [shifted(product, 2), shifted(product, 1), product]
+            convolved = taps[0] * before[0] + taps[1] * before[1] + taps[2] * before[2]
+            d_conv = d_mix * c_now
+            for k in range(3):
+                small[0, 2 + k : 3 + k, lanes] += jnp.sum(
+                    d_conv * before[k], axis=0, keepdims=True
+                )
+            d_product = (
+                taps[2] * d_conv + taps[1] * shifted(d_conv, -1) + taps[0] * shifted(d_conv, -2)
+            )
+            d_proj[held, lanes] = (d_product * x_now).astype(LOW)
+            d_proj[held, features + at : features + at + width] = (d_mix * convolved).astype(LOW)
+            d_proj[held, 2 * features + at : 2 * features + at + width] = (
+                d_product * b_now
+            ).astype(LOW)
+        if part == 0:
+            w_out.to_cross()
+        if part == 1:
+            for copy in up_loads:
+                copy.wait()
+            up.combine_all()
+
+    for turn in (3, 1):
+        w_in.compute(turn, act_one, d_proj)
+        w_in.to_core(turn)
+    for turn in (2, 0):
+        w_in.compute(turn, act_one, d_proj)
+    w_in.to_cross()
+    down_share = Share(copies, local, down.total(), lambda at: down_sum.at[at])
+    w_out.near_all()
+
+    for start in range(0, rows, slot):
+        held = slice(start, start + slot)
+        d_now = dot_last(d_proj[held], v_in[...].reshape(features, 3 * features))
+        values = rows_ref[held].astype(F32)
+        scale = rms_scale(values)
+        small[0, 0:1] += jnp.sum(d_now * values * scale, axis=0, keepdims=True)
+        d_hstate[held] += norm_back(d_now, values, scale, gain_one)
+    d_out = local.copy(d_hstate, d_rows_ref)
+    gate_share = Share(copies, local, gate.total(), lambda at: gate_sum.at[at])
+    w_out.combine_all()
+
+    hops = [(0, 1), *[(0, bit) for bit in bits], (1, 0), (2, 0)]
+    for step, (rep_bits, place_bits) in enumerate(hops):
+        copies.send(small.at[step], small_in.at[step], rep_bits, place_bits).wait_recv()
+        small[step + 1] = small[step] + small_in[step]
+    small_sum[...] = small[len(hops)]
+
+    ffn_near[1].wait_recv()
+    up_share = Share(copies, local, up.total(), lambda at: up_sum.at[at])
+
+    def columns(target, width):
+        return lambda at: target.at[:, pl.ds(pl.multiple_of(at * width, width), width)]
+
+    out_share = Share(
+        copies, local, w_out.collect.total(), columns(out_sum, features // 4)
+    )
+    down_share.forward()
+    gate_share.forward()
+    w_in.near_all()
+    w_in.combine_all()
+
+    ffn_across.wait_recv()
+    for source in (ffn_ref.at[0], ffn_in.at[0], ffn_in.at[2]):
+        load = local.copy(source, d_act.at[0])
+        load.wait()
+        add_into(hstate, d_act.at[0])
+    put_out = local.copy(hstate, outputs_ref)
+    in_share = Share(
+        copies, local, w_in.collect.total(), columns(in_sum, 3 * features // 4)
+    )
+    shares = [down_share, gate_share, up_share, out_share, in_share]
+    for share in shares[2:]:
+        share.forward()
+    for share in shares:
+        share.finish()
+    put_out.wait()
+    d_out.wait()
+    copies.close()
+
+
+def run_backward(rows, cot, gains, m_in, m_out, d_act, ffn, down, gate, up, slot):
+    count, features = rows.shape
+    shards, cut = down.shape[:2]
+    part = m_in.shape[1]
+    half = shards // 2
+    hbm = pl.BlockSpec(memory_space=pltpu.HBM)
+    vmem = pl.BlockSpec(memory_space=pltpu.VMEM)
+    hops = 10 * shards + 40
+    depth = shards.bit_length() + 1
+
+    def blocks(shape):
+        return [
+            pltpu.VMEM((half, *shape), LOW),
+            pltpu.VMEM((half, *shape), LOW),
+            pltpu.VMEM((max(half - 1, 1), *shape), LOW),
+        ]
+
+    def quarters(width):
+        return [
+            pltpu.VMEM((4, shards, part, width), LOW),
+            pltpu.VMEM((2, shards, part, width), LOW),
+            pltpu.VMEM((shards, part, width), LOW),
+            *blocks((part, width))[1:],
+        ]
+
+    whole = (count, features)
+    return pl.pallas_call(
+        functools.partial(backward_kernel, slot),
+        out_shape=[
+            jax.ShapeDtypeStruct(*shape)
+            for shape in (
+                (whole, F32),
+                (whole, F32),
+                ((4, *down.shape[1:]), LOW),
+                ((4, *gate.shape[1:]), LOW),
+                ((4, *up.shape[1:]), LOW),
+                ((part, 3 * features), LOW),
+                ((part, features), LOW),
+                ((8, features), F32),
+                ((3, *whole), LOW),
+            )
+        ],
+        in_specs=[vmem, hbm, vmem] + [hbm] * 7,
+        out_specs=[hbm] * 7 + [vmem, hbm],
+        scratch_shapes=[
+            pltpu.VMEM(m_in.shape, LOW),
+            pltpu.VMEM(m_out.shape, LOW),
+            pltpu.VMEM(whole, LOW),
+            pltpu.VMEM(whole, F32),
+            pltpu.VMEM(whole, F32),
+            pltpu.VMEM(whole, F32),
+            pltpu.VMEM(whole, LOW),
+            pltpu.VMEM(whole, F32),
+            pltpu.VMEM((2, *whole), LOW),
+            pltpu.VMEM((2, *whole), LOW),
+            pltpu.VMEM(whole, LOW),
+            pltpu.VMEM(whole, LOW),
+            pltpu.VMEM(whole, F32),
+            pltpu.VMEM(whole, LOW),
+            pltpu.VMEM((count, 3 * features), LOW),
+            *blocks(down.shape[1:]),
+            *blocks(gate.shape[1:]),
+            *blocks(up.shape[1:]),
+            *quarters(features // 4),
+            *quarters(3 * features // 4),
+            pltpu.VMEM((depth + 1, 8, features), F32),
+            pltpu.VMEM((depth, 8, features), F32),
+            pltpu.SemaphoreType.DMA((hops,)),
+            pltpu.SemaphoreType.DMA((hops,)),
+            pltpu.SemaphoreType.DMA((2 * shards + 24,)),
+        ],
+        compiler_params=pltpu.CompilerParams(
+            collective_id=1, has_side_effects=True, vmem_limit_bytes=63 << 20
+        ),
+        name="backward",
+    )(rows, cot, gains, m_in, m_out, d_act, ffn, down, gate, up)
+
+
 def on_device(
     inputs, cotangent, lengths, norm_one, w_in, conv_w, w_out, norm_two, w_gate, w_up, w_down
 ):
@@ -481,138 +793,78 @@
     place = lax.axis_index("fsdp")
     rep = lax.axis_index("rep")
     all_rows = micro_count * tok_rows
-    hidden_own = w_down.shape[0]
-    cut = hidden_own // 4
+    cut = w_down.shape[0] // 4
+    part = w_in.shape[0]
     part_ff = shards * cut
 
     slot_cols = jnp.arange(lengths.shape[1], dtype=jnp.int32)
     slot_id = rep * shards + place
     length_now = jnp.sum(jnp.where(slot_cols == slot_id, lengths, 0), axis=1)
     position = jnp.arange(tok_rows, dtype=jnp.int32)
-    live = (position[None] < length_now[:, None]).astype(F32)[..., None]
-    cotan_f = (cotangent.astype(F32) * live).reshape(all_rows, features)
-    cotan_low = cotan_f.astype(LOW)
+    live = (position[None] < length_now[:, None])[..., None]
+    cot = jnp.where(live, cotangent, jnp.zeros_like(cotangent)).reshape(all_rows, features)
 
     small = jnp.concatenate([norm_one[None], norm_two[None], conv_w, jnp.zeros_like(conv_w)])
     small = lax.dynamic_update_slice(
-        jnp.zeros((8, features), F32), small.astype(F32), (0, place * small.shape[1])
+        jnp.zeros((8, features), F32), small.astype(F32), (0, place * part)
     )
-    gate_own = lax.dynamic_index_in_dim(
-        w_gate.reshape(-1, shards, 4, cut), rep, 2, keepdims=False
-    ).reshape(-1, part_ff)
-    up_own = lax.dynamic_index_in_dim(
-        w_up.reshape(-1, shards, 4, cut), rep, 2, keepdims=False
-    ).reshape(-1, part_ff)
+
+    def unit_quarter(weight):
+        return lax.dynamic_index_in_dim(
+            weight.reshape(-1, shards, 4, cut), rep, 2, keepdims=False
+        ).reshape(-1, part_ff)
+
     down_own = lax.dynamic_slice_in_dim(w_down, rep * cut, cut, 0)
     rows_low = inputs.reshape(all_rows, features)
     m_in, m_out, m_gate, m_up, m_down, act_all, cot_all, gains = run_forward(
-        rows_low, cotan_low, small, w_in, w_out, gate_own, up_own, down_own, tok_rows
+        rows_low, cot, small, w_in, w_out, unit_quarter(w_gate), unit_quarter(w_up), down_own,
+        tok_rows,
     )
-    m_in = m_in.reshape(features, -1)
-    m_out = m_out.reshape(features, -1)
     m_gate = m_gate.reshape(features, part_ff)
     m_up = m_up.reshape(features, part_ff)
     m_down = m_down.reshape(part_ff, features)
-    g_one, g_two, taps = gains[0], gains[1], gains[2:5]
-    act_near, act_far = act_all[:2].reshape(-1, features), act_all[2:].reshape(-1, features)
-    cot_near, cot_far = cot_all[:2].reshape(-1, features), cot_all[2:].reshape(-1, features)
-
-    rows_f = inputs.reshape(all_rows, features).astype(F32)
-    scale_one = rms_scale(rows_f)
-    act_one = (rows_f * scale_one * g_one).astype(LOW)
-    projected = dot(act_one, m_in)
-    part_b = projected[:, :features]
-    part_c = projected[:, features : 2 * features]
-    part_x = projected[:, 2 * features :]
-    product = (part_b * part_x).reshape(micro_count, tok_rows, features)
-    padded = jnp.pad(product, ((0, 0), (2, 0), (0, 0)))
-    convolved = (
-        taps[0] * padded[:, :-2] + taps[1] * padded[:, 1:-1] + taps[2] * padded[:, 2:]
-    ).reshape(all_rows, features)
-    mixer_in = (part_c * convolved).astype(LOW)
-    hstate = rows_f + dot(mixer_in, m_out)
-    scale_two = rms_scale(hstate)
-    act_two = (hstate * scale_two * g_two).astype(LOW)
-
-    def units(act, cot):
-        gate_pre = dot(act, m_gate)
-        up_pre = dot(act, m_up)
-        sigmoid_g = jax.nn.sigmoid(gate_pre)
-        silu_g = gate_pre * sigmoid_g
-        hidden = (silu_g * up_pre).astype(LOW)
-        d_hidden = dot_last(cot, m_down)
-        d_gate = (d_hidden * up_pre * sigmoid_g * (1.0 + gate_pre * (1.0 - sigmoid_g))).astype(LOW)
-        d_up = (d_hidden * silu_g).astype(LOW)
-        return hidden, d_gate, d_up
-
-    hidden_n, d_gate_n, d_up_n = units(act_near, cot_near)
-    hidden_f, d_gate_f, d_up_f = units(act_far, cot_far)
-    grad_down = dot_first(hidden_n, cot_near) + dot_first(hidden_f, cot_far)
-    d_act_two = sum_over_rep(
-        dot_last(d_gate_n, m_gate) + dot_last(d_up_n, m_up),
-        dot_last(d_gate_f, m_gate) + dot_last(d_up_f, m_up),
+    act = act_all.reshape(-1, features)
+    cots = cot_all.reshape(-1, features)
+
+    gate_pre = dot(act, m_gate)
+    up_pre = dot(act, m_up)
+    sigmoid_g = jax.nn.sigmoid(gate_pre)
+    silu_g = gate_pre * sigmoid_g
+    hidden = (silu_g * up_pre).astype(LOW)
+    d_hidden = dot_last(cots, m_down)
+    d_gate = (d_hidden * up_pre * sigmoid_g * (1.0 + gate_pre * (1.0 - sigmoid_g))).astype(LOW)
+    d_up = (d_hidden * silu_g).astype(LOW)
+    d_act = (dot_last(d_gate, m_gate) + dot_last(d_up, m_up)).astype(LOW)
+    ffn = dot(hidden, m_down).astype(LOW)
+    grad_down = dot_first(hidden, cots).astype(LOW)
+    grad_gate = dot_first(act, d_gate).astype(LOW)
+    grad_up = dot_first(act, d_up).astype(LOW)
+
+    outputs, d_rows, down_sum, gate_sum, up_sum, in_sum, out_sum, small_sum, _ = run_backward(
+        rows_low, cot, gains, m_in, m_out,
+        d_act.reshape(4, all_rows, features), ffn.reshape(4, all_rows, features),
+        grad_down.reshape(shards, cut, features),
+        grad_gate.reshape(shards, part, part_ff),
+        grad_up.reshape(shards, part, part_ff),
+        tok_rows,
     )
-    grad_gate = dot_first(act_near, d_gate_n) + dot_first(act_far, d_gate_f)
-    grad_up = dot_first(act_near, d_up_n) + dot_first(act_far, d_up_f)
-    ffn = sum_over_rep(dot(hidden_n, m_down), dot(hidden_f, m_down))
-    outputs = (hstate + ffn).reshape(inputs.shape)
-
-    sum_down = reduce_pieces(grad_down.reshape(shards, cut, features))
-    sum_gate = reduce_pieces(grad_gate.reshape(shards, -1, part_ff))
-    sum_up = reduce_pieces(grad_up.reshape(shards, -1, part_ff))
-    all_down = share_quarters(sum_down.astype(LOW)).reshape(hidden_own, features).astype(F32)
-
-    def unit_columns(total):
-        quarters = share_quarters(total.astype(LOW)).reshape(4, -1, shards, cut)
-        return quarters.transpose(1, 2, 0, 3).reshape(-1, 4 * part_ff).astype(F32)
-
-    all_gate = unit_columns(sum_gate)
-    all_up = unit_columns(sum_up)
-
-    grad_two = jnp.sum(d_act_two * hstate * scale_two, axis=0)
-    d_hstate = cotan_f + norm_back(d_act_two, hstate, scale_two, g_two)
-    d_mixer = d_hstate.astype(LOW)
-    grad_out = dot_first(mixer_in, d_mixer)
-    d_mixin = dot_last(d_mixer, m_out)
-    d_cpart = d_mixin * convolved
-    d_conv = (d_mixin * part_c).reshape(micro_count, tok_rows, features)
-    trailing = jnp.pad(d_conv, ((0, 0), (0, 2), (0, 0)))
-    d_product = (
-        taps[2] * d_conv + taps[1] * trailing[:, 1:-1] + taps[0] * trailing[:, 2:]
-    ).reshape(all_rows, features)
-    grad_conv = [
-        jnp.sum(d_conv * padded[:, k : k + tok_rows], axis=(0, 1)) for k in range(3)
-    ]
-    d_projected = jnp.concatenate(
-        [d_product * part_x, d_cpart, d_product * part_b], axis=1
-    ).astype(LOW)
-    grad_in = dot_first(act_one, d_projected)
-    d_act_one = dot_last(d_projected, m_in)
-    grad_one = jnp.sum(d_act_one * rows_f * scale_one, axis=0)
-    d_rows = d_hstate + norm_back(d_act_one, rows_f, scale_one, g_one)
-    d_inputs = d_rows.reshape(inputs.shape)
-
-    all_out = reduce_full(grad_out)
-    all_in = reduce_full(grad_in)
-
-    zeros = jnp.zeros_like(grad_one)
-    small_grads = jnp.stack([grad_one, grad_two, *grad_conv, zeros, zeros, zeros])
-    small_grads = jnp.moveaxis(small_grads.reshape(8, shards, -1), 1, 0)
-    small_own = reduce_pieces(small_grads, F32)
-    small_own = small_own + hop(small_own, "rep", 1)
-    small_own = small_own + hop(small_own, "rep", 2)
-
+
+    def unit_columns(quarters):
+        quarters = quarters.reshape(4, part, shards, cut)
+        return quarters.transpose(1, 2, 0, 3).reshape(part, 4 * part_ff).astype(F32)
+
+    small_own = lax.dynamic_slice_in_dim(small_sum, place * part, part, 1)
     return (
-        outputs,
-        d_inputs,
+        outputs.reshape(inputs.shape),
+        d_rows.reshape(inputs.shape),
         small_own[0],
-        all_in,
+        in_sum.astype(F32),
         small_own[2:5],
-        all_out,
+        out_sum.astype(F32),
         small_own[1],
-        all_gate,
-        all_up,
-        all_down,
+        unit_columns(gate_sum),
+        unit_columns(up_sum),
+        down_sum.reshape(4 * cut, features).astype(F32),
     )
 
 

time: 587 us -> 425 us (0.72)
  the two profiles are of different devices: /device:TPU:0 before, /device:TPU:9 now
where the time goes in v3:
time: 425 us; the launch traced here: 416 us
  Pallas kernels  302 us (71%)
  matrix products  79.9 us (19%)
  local copies, waits for them, and re-layouts  22.8 us (5%)
  other arithmetic  10.7 us (3%)
    pallas_call x1, Pallas kernels, run_backward(): pl.pallas_call(functools.partial(backward_kernel, slot), out_shape=[jax.S...  177 us
    pallas_call x1, Pallas kernels, run_forward(): pl.pallas_call(functools.partial(forward_kernel, slot), out_shape=[jax.Sh...  125 us
    dot_general x3, matrix products, dot(): return jnp.dot(left, right, preferred_element_type=F32)  32.5 us
    dot_general x3, matrix products, dot_last(): lax.dot_general(left, right, (((1,), (1,)), ((), ())), preferred_element_...  23.9 us
    dot_general x3, matrix products, dot_first(): lax.dot_general(left, right, (((0,), (0,)), ((), ())), preferred_element_...  23.4 us
    unnamed x38, local copies, waits for them, and re-layouts  11.4 us

profile of v3, /device:TPU:9, one launch (start us, length us, event | category | flops | bytes accessed | tf_op | source)
XLA Modules:
  0.0 416.3 jit_solution(15141963046376646325)
XLA Ops:
  0.7 0.9 select_reduce_fusion
  1.7 0.6 broadcast_in_dim.38
  2.3 1.4 convert_dynamic-update-slice_fusion.small_ref
  3.7 1.7 constant_dynamic-slice_fusion.1.down_ref
  5.4 2.3 broadcast_select_fusion
  7.7 1.7 copy.25
  9.4 0.7 copy.26
  10.2 0.9 copy.28.up_ref
  11.1 0.9 copy.27.gate_ref
  12.0 125.4 %forward.1 = (bf16[8,128,3072]{2,1,0:T(8,128)(2,1)}, bf16[8,128,1024]{2,1,0:T(8,128)(2,1)}, bf16[8,128,1152]{2,1,0:T(8,128)(2,1)}, bf16[8,128,1152]{2,1,0:T(8,12...) custom-call(bf16[512,1024]{1,0:T(8,128)(2,1)} %bitcast.61, ...), custom_call_target="tpu_custom_call" | custom-call | tf_op jit(solution)/shard_map/forward/pallas_call | solution.py:332
  137.5 10.5 %fusion.1 = f32[2048,1152]{1,0:T(8,128)} fusion(bf16[2048,1024]{1,0:T(8,128)(2,1)} %bitcast.78, bf16[1152,1024]{1,0:T(8,128)(2,1)} %bitcast.84), kind=kOutput, calls=%fused_computation.22 | convolution fusion | flops 4831838208 | bytes 15990784 | tf_op jit(solution)/shard_map/dot_general | solution.py:25
  148.0 7.9 %fusion.2 = f32[2048,1152]{1,0:T(8,128)} fusion(bf16[2048,1024]{1,0:T(8,128)(2,1)S(1)} %bitcast.74, bf16[1024,1152]{1,0:T(8,128)(2,1)S(1)} %bitcast.82), kind=kOutput, calls=%fused_computation.23 | convolution fusion | flops 4831838208 | bytes 15990784 | tf_op jit(solution)/shard_map/dot_general | solution.py:21
  155.9 17.5 %multiply_convert_fusion = (bf16[2048,1152]{1,0:T(8,128)(2,1)}, bf16[2048,1152]{1,0:T(8,128)(2,1)}, bf16[2048,1152]{1,0:T(8,128)(2,1)}) fusion(f32[2048,1152]{1,0:T(8,128)} %fusion.2, f32[2048,1152]{1,0:T(8,128)} %fusion.1, bf16[2048,1024]{1,0:T(8,128)(2,1)S(1)} %bitcast.75, bf16[1024,1152]{1,0:T(8,128)(2,1)S(1)} %bitcast.80), kind=kOutput, calls=%fused_computation | convolution fusion | flops 4867227648 | bytes 39583744 | tf_op jit(solution)/shard_map/dot_general | solution.py:21
  173.5 8.9 %convolution_convert_fusion.2 = bf16[1152,1024]{1,0:T(8,128)(2,1)} fusion(bf16[2048,1152]{1,0:T(8,128)(2,1)} %get-tuple-element.52, bf16[2048,1024]{1,0:T(8,128)(2,1)S(1)} %bitcast.79), kind=kOutput, calls=%fused_computation.8 | convolution fusion | flops 4833017856 | bytes 11272192 | tf_op jit(solution)/shard_map/dot_general | solution.py:29
  182.3 7.1 %convolution_convert_fusion.3 = bf16[2048,1024]{1,0:T(8,128)(2,1)} fusion(bf16[2048,1152]{1,0:T(8,128)(2,1)S(1)} %copy-done.11, bf16[1152,1024]{1,0:T(8,128)(2,1)S(1)} %bitcast.85), kind=kOutput, calls=%fused_computation.9 | convolution fusion | flops 4833935360 | bytes 11272192 | tf_op jit(solution)/shard_map/dot_general | solution.py:21
  189.4 7.1 %convolution_convert_fusion.1 = bf16[1024,1152]{1,0:T(8,128)(2,1)} fusion(bf16[2048,1024]{1,0:T(8,128)(2,1)S(1)} %bitcast.76, bf16[2048,1152]{1,0:T(8,128)(2,1)S(1)} %bitcast.89), kind=kOutput, calls=%fused_computation.7 | convolution fusion | flops 4833017856 | bytes 11272192 | tf_op jit(solution)/shard_map/dot_general | solution.py:29
  196.5 7.5 %convolution_convert_fusion = bf16[1024,1152]{1,0:T(8,128)(2,1)} fusion(bf16[2048,1024]{1,0:T(8,128)(2,1)S(1)} %bitcast.77, bf16[2048,1152]{1,0:T(8,128)(2,1)S(1)} %bitcast.87), kind=kOutput, calls=%fused_computation.6 | convolution fusion | flops 4833017856 | bytes 11272192 | tf_op jit(solution)/shard_map/dot_general | solution.py:29
  204.0 5.8 %fusion.3 = f32[2048,1024]{1,0:T(8,128)S(1)} fusion(bf16[2048,1152]{1,0:T(8,128)(2,1)S(1)} %bitcast.89, bf16[1024,1152]{1,0:T(8,128)(2,1)S(1)} %bitcast.83), kind=kOutput, calls=%fused_computation.24 | convolution fusion | flops 4831838208 | bytes 15466496 | tf_op jit(solution)/shard_map/dot_general | solution.py:25
  209.8 7.6 %add_convert_fusion = bf16[2048,1024]{1,0:T(8,128)(2,1)} fusion(f32[2048,1024]{1,0:T(8,128)S(1)} %fusion.3, bf16[2048,1152]{1,0:T(8,128)(2,1)S(1)} %bitcast.87, bf16[1024,1152]{1,0:T(8,128)(2,1)S(1)} %bitcast.81), kind=kOutput, calls=%fused_computation.5 | convolution fusion | flops 4836032512 | bytes 19660800 | tf_op jit(solution)/shard_map/dot_general | solution.py:25
  217.5 176.6 %backward.1 = (f32[512,1024]{1,0:T(8,128)}, f32[512,1024]{1,0:T(8,128)}, bf16[4,144,1024]{2,1,0:T(8,128)(2,1)}, bf16[4,128,1152]{2,1,0:T(8,128)(2,1)}, bf16[4,12...) custom-call(bf16[512,1024]{1,0:T(8,128)(2,1)} %bitcast.62, ...), custom_call_target="tpu_custom_call" | custom-call | tf_op jit(solution)/shard_map/backward/pallas_call | solution.py:736
  394.0 0.7 constant_dynamic-slice_fusion
  395.8 1.8 convert_element_type.73
  397.6 2.4 convert_element_type.72
  400.0 1.6 copy.29
  401.6 1.6 copy.30
  403.2 3.0 copy.33
  406.3 0.6 copy.31
  406.9 1.6 copy.32
  408.5 3.2 copy.34
  411.7 1.8 bitcast_convert_fusion
  413.5 1.3 copy.38
  414.8 1.3 copy.39
  (41 shorter events, 1.4 us)
Async XLA Ops:
  0.6 8.8 %copy-start.4 = (bf16[128,4608]{1,0:T(8,128)(2,1)S(1)}, bf16[128,4608]{1,0:T(8,128)(2,1)}, u32[]{:S(2)}) copy-start(bf16[128,4608]{1,0:T(8,128)(2,1)} %param.20) | copy-start | bytes 3538948
  137.5 10.5 %copy-start.5 = (bf16[4,512,1024]{2,1,0:T(8,128)(2,1)S(1)}, bf16[4,512,1024]{2,1,0:T(8,128)(2,1)}, u32[]{:S(2)}) copy-start(bf16[4,512,1024]{2,1,0:T(8,128)(2,1)} %get-tuple-element.31) | copy-start | bytes 12582916
  137.5 10.5 %copy-start.8 = (bf16[8,128,1152]{2,1,0:T(8,128)(2,1)S(1)}, bf16[8,128,1152]{2,1,0:T(8,128)(2,1)}, u32[]{:S(2)}) copy-start(bf16[8,128,1152]{2,1,0:T(8,128)(2,1)} %get-tuple-element.33) | copy-start | bytes 7077892
  148.0 7.9 %copy-start.7 = (bf16[8,128,1152]{2,1,0:T(8,128)(2,1)S(1)}, bf16[8,128,1152]{2,1,0:T(8,128)(2,1)}, u32[]{:S(2)}) copy-start(bf16[8,128,1152]{2,1,0:T(8,128)(2,1)} %get-tuple-element.32) | copy-start | bytes 7077892
  155.9 17.5 %copy-start.6 = (bf16[4,512,1024]{2,1,0:T(8,128)(2,1)S(1)}, bf16[4,512,1024]{2,1,0:T(8,128)(2,1)}, u32[]{:S(2)}) copy-start(bf16[4,512,1024]{2,1,0:T(8,128)(2,1)} %get-tuple-element.29) | copy-start | bytes 12582916
  173.4 8.9 %copy-start.10 = (bf16[8,144,1024]{2,1,0:T(8,128)(2,1)S(1)}, bf16[8,144,1024]{2,1,0:T(8,128)(2,1)}, u32[]{:S(2)}) copy-start(bf16[8,144,1024]{2,1,0:T(8,128)(2,1)} %get-tuple-element.30) | copy-start | bytes 7077892
  173.4 8.9 %copy-start.11 = (bf16[2048,1152]{1,0:T(8,128)(2,1)S(1)}, bf16[2048,1152]{1,0:T(8,128)(2,1)}, u32[]{:S(2)}) copy-start(bf16[2048,1152]{1,0:T(8,128)(2,1)} %get-tuple-element.52) | copy-start | bytes 14155780
  173.4 16.0 %slice-start.2 = ((s8[4718592]{0:T(1024)(128)(4,1)}), s8[4194304]{0:T(1024)(128)(4,1)S(1)}, s32[]{:S(2)}) async-start(s8[4718592]{0:T(1024)(128)(4,1)} %bitcast.88), calls=%async_computation.2 | async-start | bytes 8388608
  173.4 23.1 %slice-start = ((s8[4718592]{0:T(1024)(128)(4,1)}), s8[4194304]{0:T(1024)(128)(4,1)S(1)}, s32[]{:S(2)}) async-start(s8[4718592]{0:T(1024)(128)(4,1)} %bitcast.86), calls=%async_computation | async-start | bytes 8388608
  182.3 7.1 %slice-start.3 = ((s8[4718592]{0:T(1024)(128)(4,1)}), s8[524288]{0:T(1024)(128)(4,1)S(1)}, s32[]{:S(2)}) async-start(s8[4718592]{0:T(1024)(128)(4,1)} %bitcast.88), calls=%async_computation.3 | async-start | bytes 1048576
  182.3 14.2 %slice-start.1 = ((s8[4718592]{0:T(1024)(128)(4,1)}), s8[524288]{0:T(1024)(128)(4,1)S(1)}, s32[]{:S(2)}) async-start(s8[4718592]{0:T(1024)(128)(4,1)} %bitcast.86), calls=%async_computation.1 | async-start | bytes 1048576
  196.5 7.5 %copy-start.9 = (bf16[8,128,1152]{2,1,0:T(8,128)(2,1)S(1)}, bf16[8,128,1152]{2,1,0:T(8,128)(2,1)}, u32[]{:S(2)}) copy-start(bf16[8,128,1152]{2,1,0:T(8,128)(2,1)} %get-tuple-element.33) | copy-start | bytes 7077892
  401.6 4.7 %copy-start.3 = (bf16[4,128,1152]{2,1,0:T(8,128)(2,1)S(1)}, bf16[4,128,1152]{2,1,0:T(8,128)(2,1)}, u32[]{:S(2)}) copy-start(bf16[4,128,1152]{2,1,0:T(8,128)(2,1)} %get-tuple-element.40) | copy-start | bytes 3538948
  406.9 4.8 %copy-start.2 = (bf16[4,144,1024]{2,1,0:T(8,128)(2,1)S(1)}, bf16[4,144,1024]{2,1,0:T(8,128)(2,1)}, u32[]{:S(2)}) copy-start(bf16[4,144,1024]{2,1,0:T(8,128)(2,1)} %get-tuple-element.41) | copy-start | bytes 3538948
  408.5 5.0 %copy-start.1 = (f32[512,1024]{1,0:T(8,128)S(1)}, f32[512,1024]{1,0:T(8,128)}, u32[]{:S(2)}) copy-start(f32[512,1024]{1,0:T(8,128)} %get-tuple-element.34) | copy-start | bytes 6291460
  411.7 3.1 copy-start
